TPU v7x, 32 devices: a whole 2x2x4 slice. The times are simulated.
32 devices in a mesh: dp: 16 (over z, y, core), tile: 2 (over x).
Axes of the slice: x: 2, y: 2, z: 4, core: 2. Of those that a mesh axis runs over, the one named last changes fastest.
Arguments:
- tokens: bfloat16 [16, 1024, 768], P('dp', 'tile'), may hold values from -11 to 11
- segment_ids: int32 [16, 1024], P('dp'), may hold values from 0 to 7, never falling along the last dimension, each value on 1 to 256 neighbouring positions
- keep_mask: int32 [16, 1024], P('dp'), may hold values 0 or 1
- gain_one: float32 [768], replicated, may hold values from 0.25 to 1.75
- bias_one: float32 [768], replicated, may hold values from -3 to 3
- qkv_weight: bfloat16 [768, 2304], replicated, may hold values from -0.21875 to 0.21875
- query_bias: float32 [768], replicated, may hold values from -3 to 3
- value_bias: float32 [768], replicated, may hold values from -3 to 3
- out_weight: bfloat16 [768, 768], replicated, may hold values from -2 to 2
- out_bias: float32 [768], replicated, may hold values from -3 to 3
- gain_two: float32 [768], replicated, may hold values from 0.25 to 1.75
- bias_two: float32 [768], replicated, may hold values from -3 to 3
- fc1_weight: bfloat16 [768, 3072], replicated, may hold values from -0.21875 to 0.21875
- fc1_bias: float32 [3072], replicated, may hold values from -3 to 3
- fc2_weight: bfloat16 [3072, 768], replicated, may hold values from -0.15625 to 0.15625
- fc2_bias: float32 [768], replicated, may hold values from -3 to 3
- cotangent: bfloat16 [16, 1024, 768], P('dp', 'tile'), may hold values from -6 to 6
Outputs:
- output: bfloat16 [16, 1024, 768], P('dp', 'tile')
- grad_tokens: bfloat16 [16, 1024, 768], P('dp', 'tile')
- gain_one_grad: float32 [768], replicated
- bias_one_grad: float32 [768], replicated
- qkv_grad: float32 [768, 2304], P('dp', 'tile')
- query_bias_grad: float32 [768], replicated
- value_bias_grad: float32 [768], replicated
- out_grad: float32 [768, 768], P('dp', 'tile')
- out_bias_grad: float32 [768], replicated
- gain_two_grad: float32 [768], replicated
- bias_two_grad: float32 [768], replicated
- fc1_grad: float32 [768, 3072], P('dp', 'tile')
- fc1_bias_grad: float32 [3072], replicated
- fc2_grad: float32 [3072, 768], P('dp', 'tile')
- fc2_bias_grad: float32 [768], replicated
- root_mean: float32 [4], replicated
Inputs may be any that keep to these rules, and one draw needn't show every extreme that they name: `segment_ids`: within a sequence the ids never fall; each of the 8 images has 1 to 256 slots, and one has exactly 256.
All inputs are finite; a program needn't handle non-finite values. No bound on the sum of `keep_mask` on one device may be relied on, other than what follows from the above.
Results may differ from a plain program's by a relative error of at most 0.017.
Values may be sent and summed in bfloat16 or wider, within the bound.
A program may use at most 192 MiB of HBM per device.

v0:
```python
import jax
import jax.numpy as jnp
from jax import lax
from jax.sharding import PartitionSpec as P

HEAD_DIM = 64


def layer_norm(values, norm_gain, norm_bias):
    average = jnp.mean(values, axis=-1, keepdims=True)
    centred = values - average
    variance = jnp.mean(centred * centred, axis=-1, keepdims=True)
    return centred * lax.rsqrt(variance + 1e-06) * norm_gain + norm_bias


def exact_gelu(values):
    return jax.nn.gelu(values, approximate=False)


def on_device(
    tokens,
    segment_ids,
    keep_mask,
    gain_one,
    bias_one,
    qkv_weight,
    query_bias,
    value_bias,
    out_weight,
    out_bias,
    gain_two,
    bias_two,
    fc1_weight,
    fc1_bias,
    fc2_weight,
    fc2_bias,
    cotangent,
):
    sequences, tile_rows, model_width = tokens.shape
    length = segment_ids.shape[1]
    count_rows = sequences * tile_rows
    head_block = 4 * HEAD_DIM
    score_scale = HEAD_DIM ** (-0.5)
    offset = lax.axis_index("tile") * tile_rows
    query_ids = lax.dynamic_slice_in_dim(segment_ids, offset, tile_rows, 1)
    query_keep = lax.dynamic_slice_in_dim(keep_mask, offset, tile_rows, 1)
    positions = offset + jnp.arange(tile_rows, dtype=jnp.int32)
    key_places = jnp.arange(length, dtype=jnp.int32)
    own_slot = positions[:, None] == key_places[None, :]
    usable = (keep_mask[:, None, :] == 1) | own_slot[None]
    allowed = ((query_ids[:, :, None] == segment_ids[:, None, :]) & usable)[:, None]
    flattened = tokens.reshape(count_rows, model_width).astype(jnp.float32)
    normed = layer_norm(flattened, gain_one, bias_one)
    normed_low = normed.astype(jnp.bfloat16)
    key_bias = jnp.zeros_like(query_bias)
    projected = jnp.dot(
        normed_low, qkv_weight, preferred_element_type=jnp.float32
    ) + jnp.concatenate([query_bias, key_bias, value_bias])
    projected_low = projected.astype(jnp.bfloat16).reshape(sequences, tile_rows, 3 * model_width)
    queries = projected_low[..., :model_width]
    shared_local = projected_low[..., model_width:]
    shared_all = lax.all_gather(shared_local, "tile", axis=1, tiled=True)
    keys_all = shared_all[..., :model_width]
    values_all = shared_all[..., model_width:]
    key_count = shared_all.shape[1]

    def split_heads(source, column):
        sliced = source[..., column : column + head_block]
        return sliced.reshape(sliced.shape[0], sliced.shape[1], 4, HEAD_DIM)

    def block_scores(query_part, key_part):
        scores = (
            jnp.einsum("sqhe,skhe->shqk", query_part, key_part, preferred_element_type=jnp.float32)
            * score_scale
        )
        return jnp.where(allowed, scores, -1e30)

    attended_parts = []
    logsums = []
    for column in range(0, model_width, head_block):
        masked = block_scores(split_heads(queries, column), split_heads(keys_all, column))
        row_peak = jnp.max(masked, axis=-1, keepdims=True)
        exponent = jnp.exp(masked - row_peak)
        row_total = jnp.sum(exponent, axis=-1, keepdims=True)
        softmax_probs = (exponent / row_total).astype(jnp.bfloat16)
        logsums.append(row_peak + jnp.log(row_total))
        attended_parts.append(
            jnp.einsum(
                "shqk,skhe->sqhe",
                softmax_probs,
                split_heads(values_all, column),
                preferred_element_type=jnp.float32,
            )
        )
    attended = jnp.concatenate(attended_parts, axis=2)
    attended_low = attended.reshape(count_rows, model_width).astype(jnp.bfloat16)
    branch_one = jnp.dot(attended_low, out_weight, preferred_element_type=jnp.float32) + out_bias
    hidden = flattened + branch_one
    normed_two = layer_norm(hidden, gain_two, bias_two)
    normed_two_low = normed_two.astype(jnp.bfloat16)
    inner = jnp.dot(normed_two_low, fc1_weight, preferred_element_type=jnp.float32) + fc1_bias
    active_low = exact_gelu(inner).astype(jnp.bfloat16)
    branch_two = jnp.dot(active_low, fc2_weight, preferred_element_type=jnp.float32) + fc2_bias
    result = hidden + branch_two
    output = result.astype(jnp.bfloat16).reshape(sequences, tile_rows, model_width)
    weighting = query_keep.reshape(count_rows, 1).astype(jnp.float32)
    squares = [
        jnp.sum(weighting * member * member)
        for member in (flattened, branch_one, branch_two, result)
    ]
    stats = jnp.stack(squares + [jnp.sum(weighting)])
    grad_result = cotangent.reshape(count_rows, model_width)
    fc2_grad = jnp.einsum("nf,nd->fd", active_low, grad_result, preferred_element_type=jnp.float32)
    fc2_bias_grad = jnp.sum(grad_result.astype(jnp.float32), axis=0)
    grad_active = jnp.einsum(
        "nd,fd->nf", grad_result, fc2_weight, preferred_element_type=jnp.float32
    )
    inner_value, gelu_back = jax.vjp(exact_gelu, inner)
    grad_inner_low = gelu_back(grad_active)[0].astype(jnp.bfloat16)
    fc1_grad = jnp.einsum(
        "nd,nf->df", normed_two_low, grad_inner_low, preferred_element_type=jnp.float32
    )
    fc1_bias_grad = jnp.sum(grad_inner_low.astype(jnp.float32), axis=0)
    grad_normed_two = jnp.einsum(
        "nf,df->nd", grad_inner_low, fc1_weight, preferred_element_type=jnp.float32
    )
    normed_again, norm_back_two = jax.vjp(layer_norm, hidden, gain_two, bias_two)
    grad_hidden_part, gain_two_grad, bias_two_grad = norm_back_two(grad_normed_two)
    grad_hidden = grad_result.astype(jnp.float32) + grad_hidden_part
    grad_branch_low = grad_hidden.astype(jnp.bfloat16)
    out_grad = jnp.einsum(
        "nd,ne->de", attended_low, grad_branch_low, preferred_element_type=jnp.float32
    )
    out_bias_grad = jnp.sum(grad_branch_low.astype(jnp.float32), axis=0)
    grad_attended_low = (
        jnp.einsum("ne,de->nd", grad_branch_low, out_weight, preferred_element_type=jnp.float32)
        .astype(jnp.bfloat16)
        .reshape(sequences, tile_rows, model_width)
    )
    query_grads = []
    key_grads = []
    value_grads = []
    for block_index, column in enumerate(range(0, model_width, head_block)):
        query_part = split_heads(queries, column)
        key_part = split_heads(keys_all, column)
        value_part = split_heads(values_all, column)
        grad_part = split_heads(grad_attended_low, column)
        masked = block_scores(query_part, key_part)
        probs_again = jnp.exp(masked - logsums[block_index])
        grad_probs = jnp.einsum(
            "sqhe,skhe->shqk", grad_part, value_part, preferred_element_type=jnp.float32
        )
        centre = jnp.sum(probs_again * grad_probs, axis=-1, keepdims=True)
        grad_scores = (probs_again * (grad_probs - centre)).astype(jnp.bfloat16)
        query_grads.append(
            jnp.einsum("shqk,skhe->sqhe", grad_scores, key_part, preferred_element_type=jnp.float32)
            * score_scale
        )
        key_grads.append(
            jnp.einsum(
                "shqk,sqhe->skhe", grad_scores, query_part, preferred_element_type=jnp.float32
            )
            * score_scale
        )
        value_grads.append(
            jnp.einsum(
                "shqk,sqhe->skhe",
                probs_again.astype(jnp.bfloat16),
                grad_part,
                preferred_element_type=jnp.float32,
            )
        )
    grad_query = jnp.concatenate(query_grads, axis=2).reshape(sequences, tile_rows, model_width)
    grad_key_full = jnp.concatenate(key_grads, axis=2).reshape(sequences, key_count, model_width)
    grad_value_full = jnp.concatenate(value_grads, axis=2).reshape(
        sequences, key_count, model_width
    )
    grad_shared_full = jnp.concatenate([grad_key_full, grad_value_full], axis=-1)
    grad_shared = lax.psum_scatter(
        grad_shared_full.astype(jnp.bfloat16), "tile", scatter_dimension=1, tiled=True
    ).astype(jnp.float32)
    grad_projected_low = (
        jnp.concatenate([grad_query, grad_shared], axis=-1)
        .astype(jnp.bfloat16)
        .reshape(count_rows, 3 * model_width)
    )
    qkv_grad = jnp.einsum(
        "nd,ne->de", normed_low, grad_projected_low, preferred_element_type=jnp.float32
    )
    column_sums = jnp.sum(grad_projected_low.astype(jnp.float32), axis=0)
    query_bias_grad = column_sums[:model_width]
    value_bias_grad = column_sums[2 * model_width :]
    grad_normed = jnp.einsum(
        "ne,de->nd", grad_projected_low, qkv_weight, preferred_element_type=jnp.float32
    )
    normed_first, norm_back_one = jax.vjp(layer_norm, flattened, gain_one, bias_one)
    grad_tokens_part, gain_one_grad, bias_one_grad = norm_back_one(grad_normed)
    grad_tokens = (
        (grad_hidden + grad_tokens_part)
        .astype(jnp.bfloat16)
        .reshape(sequences, tile_rows, model_width)
    )
    totals_small = lax.psum(
        (
            gain_one_grad,
            bias_one_grad,
            query_bias_grad,
            value_bias_grad,
            out_bias_grad,
            gain_two_grad,
            bias_two_grad,
            fc1_bias_grad,
            fc2_bias_grad,
            stats,
        ),
        ("dp", "tile"),
    )
    matrices = (qkv_grad, out_grad, fc1_grad, fc2_grad)
    row_shares = (
        lax.psum_scatter(
            matrices[0].astype(jnp.bfloat16), "dp", scatter_dimension=0, tiled=True
        ).astype(jnp.float32),
        lax.psum_scatter(
            matrices[1].astype(jnp.bfloat16), "dp", scatter_dimension=0, tiled=True
        ).astype(jnp.float32),
        lax.psum_scatter(
            matrices[2].astype(jnp.bfloat16), "dp", scatter_dimension=0, tiled=True
        ).astype(jnp.float32),
        lax.psum_scatter(
            matrices[3].astype(jnp.bfloat16), "dp", scatter_dimension=0, tiled=True
        ).astype(jnp.float32),
    )
    reduced = (
        lax.psum_scatter(
            row_shares[0].astype(jnp.bfloat16), "tile", scatter_dimension=1, tiled=True
        ).astype(jnp.float32),
        lax.psum_scatter(
            row_shares[1].astype(jnp.bfloat16), "tile", scatter_dimension=1, tiled=True
        ).astype(jnp.float32),
        lax.psum_scatter(
            row_shares[2].astype(jnp.bfloat16), "tile", scatter_dimension=1, tiled=True
        ).astype(jnp.float32),
        lax.psum_scatter(
            row_shares[3].astype(jnp.bfloat16), "tile", scatter_dimension=1, tiled=True
        ).astype(jnp.float32),
    )
    totals = totals_small[9]
    root_mean = jnp.sqrt(totals[:4] / (totals[4] * model_width))
    return (
        output,
        grad_tokens,
        totals_small[0],
        totals_small[1],
        reduced[0],
        totals_small[2],
        totals_small[3],
        reduced[1],
        totals_small[4],
        totals_small[5],
        totals_small[6],
        reduced[2],
        totals_small[7],
        reduced[3],
        totals_small[8],
        root_mean,
    )


def solution(mesh):
    placed = (
        P("dp", "tile", None),
        P("dp", None),
        P("dp", None),
        P(),
        P(),
        P(),
        P(),
        P(),
        P(),
        P(),
        P(),
        P(),
        P(),
        P(),
        P(),
        P(),
        P("dp", "tile", None),
    )
    return jax.shard_map(
        on_device,
        mesh=mesh,
        in_specs=placed,
        out_specs=(
            P("dp", "tile", None),
            P("dp", "tile", None),
            P(),
            P(),
            P("dp", "tile"),
            P(),
            P(),
            P("dp", "tile"),
            P(),
            P(),
            P(),
            P("dp", "tile"),
            P(),
            P("dp", "tile"),
            P(),
            P(),
        ),
        check_vma=False,
    )
```

profile of v0, /device:TPU:0, one launch (start us, length us, event | category | flops | bytes accessed | tf_op | source)
XLA Modules:
  0.0 602.2 jit_solution(12091611203027383656)
XLA Ops:
  27.8 37.7 %all-gather.2.cloned.1.call-done = bf16[1,1024,1536]{2,1,0:T(8,128)(2,1)} async-done(((bf16[1,512,1536]{2,1,0:T(8,128)(2,1)}), bf16[1,1024,1536]{2,1,0:T(8,128)(2,1)}) %all-gather.2.cloned.1.call-update) | async-done | bytes 3145744 | tf_op jit(solution)/shard_map/all_gather | solution.py:62
  104.3 21.1 %multiply_convert_fusion.3 = (bf16[512,3072]{1,0:T(8,128)(2,1)}, f32[512,3072]{1,0:T(8,128)}, f32[512,3072]{1,0:T(8,128)}) fusion(f32[3072]{0:T(1024)S(1)} %copy-done.61, bf16[768,3072]{1,0:T(8,128)(2,1)S(1)} %bitcast.237, f32[512,768]{1,0:T(8,128)S(1)} %get-tuple-element.48, f32[768]{0:T(1024)S(1)} %copy-done.63, f32[768]{0:T(1024)S(1)} %copy-done.58, ...), kind=kOutput, calls=%fused_computation.28 | convolution fusion | flops 2521694208 | bytes 22042624 | tf_op jit(solution)/shard_map/dot_general | solution.py:101
  125.4 8.6 %convert_reduce_fusion = (f32[3072]{0:T(1024)}, bf16[512,3072]{1,0:T(8,128)(2,1)S(1)}) fusion(f32[512,3072]{1,0:T(8,128)} %get-tuple-element.46, bf16[3072,768]{1,0:T(8,128)(2,1)S(1)} %bitcast.239, bf16[1,512,768]{2,1,0:T(8,128)(2,1)S(1)} %copy-done.23, f32[512,3072]{1,0:T(8,128)} %get-tuple-element.73, f32[3072]{0:T(1024)S(1)} %copy-done.61), kind=kOutput, calls=%fused_computation.26 | convolution fusion | flops 2442654720 | bytes 21258240 | tf_op jit(solution)/shard_map/nd,fd->nf/dot_general | solution.py:115
  137.1 4.8 fusion.44
  152.4 5.7 fusion.67
  158.1 7.0 %multiply_reduce_fusion.2 = (f32[4,512]{1,0:T(4,128)}, f32[4,512,1024]{2,1,0:T(8,128)}) fusion(f32[4,512,1024]{2,1,0:T(8,128)} %copy-done.3, f32[4,512]{1,0:T(4,128)S(1)} %copy-done.39, bf16[512,4,64]{0,2,1:T(8,128)(2,1)S(1)} %bitcast.212, bf16[1024,4,64]{0,2,1:T(8,128)(2,1)S(1)} %bitcast.223), kind=kOutput, calls=%fused_computation.8 | convolution fusion | flops 274724864 | bytes 17580032 | tf_op jit(solution)/shard_map/sqhe,skhe->shqk/dot_general | solution.py:150
  166.9 5.8 fusion.61
  172.7 7.2 %multiply_reduce_fusion = (f32[4,512]{1,0:T(4,128)}, f32[4,512,1024]{2,1,0:T(8,128)}) fusion(f32[4,512,1024]{2,1,0:T(8,128)} %copy-done.2, f32[4,512]{1,0:T(4,128)S(1)} %log_add_fusion, bf16[512,4,64]{0,2,1:T(8,128)(2,1)S(1)} %bitcast.214, bf16[1024,4,64]{0,2,1:T(8,128)(2,1)S(1)} %bitcast.221), kind=kOutput, calls=%fused_computation.2 | convolution fusion | flops 274724864 | bytes 17580032 | tf_op jit(solution)/shard_map/sqhe,skhe->shqk/dot_general | solution.py:150
  181.7 5.8 fusion.64
  187.6 7.0 %multiply_reduce_fusion.1 = (f32[4,512]{1,0:T(4,128)}, f32[4,512,1024]{2,1,0:T(8,128)}) fusion(f32[4,512,1024]{2,1,0:T(8,128)} %copy-done.1, f32[4,512]{1,0:T(4,128)S(1)} %log_add_fusion.1, bf16[512,4,64]{0,2,1:T(8,128)(2,1)S(1)} %bitcast.216, bf16[1024,4,64]{0,2,1:T(8,128)(2,1)S(1)} %bitcast.219), kind=kOutput, calls=%fused_computation.5 | convolution fusion | flops 274724864 | bytes 17580032 | tf_op jit(solution)/shard_map/sqhe,skhe->shqk/dot_general | solution.py:150
  194.7 7.0 %multiply_convert_fusion.2 = bf16[4,512,1024]{2,1,0:T(8,128)(2,1)S(1)} fusion(f32[4,512,1024]{2,1,0:T(8,128)} %get-tuple-element.79, f32[4,512,1024]{2,1,0:T(8,128)} %copy-done.3, f32[4,512]{1,0:T(4,128)} %get-tuple-element.78, f32[4,512]{1,0:T(4,128)} %log_add_fusion.2), kind=kLoop, calls=%fused_computation.7 | loop fusion | flops 8388608 | bytes 20987904 | tf_op jit(solution)/shard_map/convert_element_type | solution.py:154
  204.5 4.9 multiply_convert_fusion
  220.7 32.2 %reduce-scatter.20.cloned.1.call-done = bf16[48,768]{1,0:T(8,128)(2,1)} async-done(((bf16[768,768]{1,0:T(8,128)(2,1)}), bf16[48,768]{1,0:T(8,128)(2,1)}) %reduce-scatter.20.cloned.1.call-update) | async-done | bytes 73744 | tf_op jit(solution)/shard_map/reduce_scatter | solution.py:223
  254.7 7.2 %convolution_convert_fusion = bf16[3072,768]{1,0:T(8,128)(2,1)} fusion(bf16[512,3072]{1,0:T(8,128)(2,1)} %get-tuple-element.45, bf16[1,512,768]{2,1,0:T(8,128)(2,1)} %param.33), kind=kOutput, calls=%fused_computation.42 | convolution fusion | flops 2418278400 | bytes 8650752 | tf_op jit(solution)/shard_map/nf,nd->fd/dot_general | solution.py:113
  262.6 7.4 %convolution_convert_fusion.1 = bf16[768,3072]{1,0:T(8,128)(2,1)} fusion(bf16[512,3072]{1,0:T(8,128)(2,1)} %copy-done.66, f32[512,768]{1,0:T(8,128)} %copy-done.11, f32[768]{0:T(1024)S(1)} %copy-done.64, f32[768]{0:T(1024)S(1)} %copy-done.59, f32[512]{0:T(512)S(1)} %copy-done.56, f32[512]{0:T(512)S(1)} %copy-done.49), kind=kOutput, calls=%fused_computation.43 | convolution fusion | flops 2420244480 | bytes 9447424 | tf_op jit(solution)/shard_map/nd,nf->df/dot_general | solution.py:120
  279.1 18.5 %reduce-scatter.16.cloned.1.call-done = bf16[1,512,1536]{1,2,0:T(8,128)(2,1)} async-done(((bf16[1,1024,1536]{1,2,0:T(8,128)(2,1)}), bf16[1,512,1536]{1,2,0:T(8,128)(2,1)}) %reduce-scatter.16.cloned.1.call-update) | async-done | bytes 1572880 | tf_op jit(solution)/shard_map/reduce_scatter | solution.py:179
  297.5 6.0 convolution_convert_fusion.2
  303.6 7.7 %reduce-scatter.30.cloned.1.call-done = bf16[384,48]{1,0:T(8,128)(2,1)} async-done(((bf16[768,48]{1,0:T(8,128)(2,1)}), bf16[384,48]{1,0:T(8,128)(2,1)}) %reduce-scatter.30.cloned.1.call-update) | async-done | bytes 36880
  314.2 76.8 %reduce-scatter.26.cloned.1.call-done = bf16[192,768]{1,0:T(8,128)(2,1)} async-done(((bf16[3072,768]{1,0:T(8,128)(2,1)}), bf16[192,768]{1,0:T(8,128)(2,1)}) %reduce-scatter.26.cloned.1.call-update) | async-done | bytes 294928 | tf_op jit(solution)/shard_map/reduce_scatter | solution.py:229
  393.0 5.6 fusion.98
  401.2 68.2 %reduce-scatter.22.cloned.1.call-done = bf16[48,3072]{1,0:T(8,128)(2,1)} async-done(((bf16[768,3072]{1,0:T(8,128)(2,1)}), bf16[48,3072]{1,0:T(8,128)(2,1)}) %reduce-scatter.22.cloned.1.call-update) | async-done | bytes 294928 | tf_op jit(solution)/shard_map/reduce_scatter | solution.py:226
  476.1 4.8 convert_reduce_fusion.2
  480.9 59.9 %reduce-scatter.18.cloned.1.call-done = bf16[48,2304]{1,0:T(8,128)(2,1)} async-done(((bf16[768,2304]{1,0:T(8,128)(2,1)}), bf16[48,2304]{1,0:T(8,128)(2,1)}) %reduce-scatter.18.cloned.1.call-update) | async-done | bytes 221200 | tf_op jit(solution)/shard_map/reduce_scatter | solution.py:220
  543.5 41.5 %all-reduce = (f32[768]{0:T(1024)}, f32[768]{0:T(1024)}, f32[768]{0:T(1024)}, f32[768]{0:T(1024)}, f32[768]{0:T(1024)}, /*index=5*/f32[768]{0:T(1024)}, f32[768]...) all-reduce(f32[768]{0:T(1024)} %get-tuple-element.18, ...), channel_id=1, replica_groups=mesh['dp'=16,'tile'=2] {'dp','tile'}, use_global_device_ids=true, to_apply=%region_19.20 | all-reduce | flops 9221 | bytes 73768 | tf_op jit(solution)/shard_map/psum | solution.py:203
  (260 shorter events, 127.9 us)
Async XLA Ops:
  7.2 58.2 %all-gather.2.cloned.1.call-start = ((), (), s32[]{:S(2)}) async-start(), calls=%async_computation.9 | async-start | bytes 4718592 | tf_op jit(solution)/shard_map/all_gather | solution.py:62
  16.3 8.8 %copy-start.53 = (s32[1,1024]{1,0:T(1,128)S(1)}, s32[1,1024]{1,0:T(1,128)}, u32[]{:S(2)}) copy-start(s32[1,1024]{1,0:T(1,128)} %param.18) | copy-start | bytes 12292
  16.3 8.8 %copy-start.54 = (s32[1,1024]{1,0:T(1,128)S(1)}, s32[1,1024]{1,0:T(1,128)}, u32[]{:S(2)}) copy-start(s32[1,1024]{1,0:T(1,128)} %param.19) | copy-start | bytes 12292
  17.6 235.3 %reduce-scatter.20.cloned.1.call-start = ((), (), s32[]{:S(2)}) async-start(), calls=%async_computation.12 | async-start | bytes 1253376 | tf_op jit(solution)/shard_map/reduce_scatter | solution.py:223
  101.9 23.5 %slice-start.6 = ((s8[4718592]{0:T(1024)(128)(4,1)}), s8[4194304]{0:T(1024)(128)(4,1)S(1)}, s32[]{:S(2)}) async-start(s8[4718592]{0:T(1024)(128)(4,1)} %bitcast.238), calls=%async_computation.25 | async-start | bytes 8388608
  103.9 38.0 %copy-start.11 = (f32[512,768]{1,0:T(8,128)}, f32[512,768]{1,0:T(8,128)S(1)}, u32[]{:S(2)}) copy-start(f32[512,768]{1,0:T(8,128)S(1)} %get-tuple-element.48) | copy-start | bytes 4718596
  103.9 38.0 %copy-start.48 = (f32[512]{0:T(512)}, f32[512]{0:T(512)S(1)}, u32[]{:S(2)}) copy-start(f32[512]{0:T(512)S(1)} %broadcast_multiply_fusion) | copy-start | bytes 6148
  104.3 37.6 %copy-start.55 = (f32[512]{0:T(512)}, f32[512]{0:T(512)S(1)}, u32[]{:S(2)}) copy-start(f32[512]{0:T(512)S(1)} %fusion.91) | copy-start | bytes 6148
  104.3 21.1 %copy-start.23 = (bf16[1,512,768]{2,1,0:T(8,128)(2,1)S(1)}, bf16[1,512,768]{2,1,0:T(8,128)(2,1)}, u32[]{:S(2)}) copy-start(bf16[1,512,768]{2,1,0:T(8,128)(2,1)} %param.33) | copy-start | bytes 2359300
  104.3 21.1 %slice-start.7 = ((s8[4718592]{0:T(1024)(128)(4,1)}), s8[524288]{0:T(1024)(128)(4,1)S(1)}, s32[]{:S(2)}) async-start(s8[4718592]{0:T(1024)(128)(4,1)} %bitcast.238), calls=%async_computation.26 | async-start | bytes 1048576
  194.6 102.9 %reduce-scatter.16.cloned.1.call-start = ((), (), s32[]{:S(2)}) async-start(), calls=%async_computation.10 | async-start | bytes 4718592 | tf_op jit(solution)/shard_map/reduce_scatter | solution.py:179
  194.7 9.1 %slice-start.2 = ((s8[8388608]{0:T(1024)(128)(4,1)}), s8[4194304]{0:T(1024)(128)(4,1)S(1)}, s32[]{:S(2)}) async-start(s8[8388608]{0:T(1024)(128)(4,1)} %bitcast.190), calls=%async_computation.21 | async-start | bytes 8388608
  194.7 9.8 %slice-start.3 = ((s8[8388608]{0:T(1024)(128)(4,1)}), s8[4194304]{0:T(1024)(128)(4,1)S(1)}, s32[]{:S(2)}) async-start(s8[8388608]{0:T(1024)(128)(4,1)} %bitcast.190), calls=%async_computation.22 | async-start | bytes 8388608
  220.7 90.6 %reduce-scatter.30.cloned.1.call-start = ((), (), s32[]{:S(2)}) async-start(), calls=%async_computation.17 | async-start | bytes 294912
  254.6 136.4 %reduce-scatter.26.cloned.1.call-start = ((), (), s32[]{:S(2)}) async-start(), calls=%async_computation.15 | async-start | bytes 5013504 | tf_op jit(solution)/shard_map/reduce_scatter | solution.py:229
  261.9 207.5 %reduce-scatter.22.cloned.1.call-start = ((), (), s32[]{:S(2)}) async-start(), calls=%async_computation.13 | async-start | bytes 5013504 | tf_op jit(solution)/shard_map/reduce_scatter | solution.py:226
  270.0 270.9 %reduce-scatter.18.cloned.1.call-start = ((), (), s32[]{:S(2)}) async-start(), calls=%async_computation.11 | async-start | bytes 3760128 | tf_op jit(solution)/shard_map/reduce_scatter | solution.py:220
  274.0 23.5 %copy-start.43 = (f32[512]{0:T(512)S(1)}, f32[512]{0:T(512)}, u32[]{:S(2)}) copy-start(f32[512]{0:T(512)} %copy-done.42) | copy-start | bytes 6148
  274.0 23.5 %copy-start.46 = (f32[512]{0:T(512)S(1)}, f32[512]{0:T(512)}, u32[]{:S(2)}) copy-start(f32[512]{0:T(512)} %copy-done.45) | copy-start | bytes 6148
  274.0 23.5 %copy-start.52 = (f32[768]{0:T(1024)S(1)}, f32[768]{0:T(1024)}, u32[]{:S(2)}) copy-start(f32[768]{0:T(1024)} %param.20) | copy-start | bytes 9220
  274.0 23.5 %copy-start.65 = (f32[768]{0:T(1024)S(1)}, f32[768]{0:T(1024)}, u32[]{:S(2)}) copy-start(f32[768]{0:T(1024)} %param.21) | copy-start | bytes 9220
  303.5 283.2 %reduce-scatter.32.cloned.1.call-start = ((), (), s32[]{:S(2)}) async-start(), calls=%async_computation.18 | async-start | bytes 589824
  392.9 197.2 %reduce-scatter.24.cloned.1.call-start = ((), (), s32[]{:S(2)}) async-start(), calls=%async_computation.14 | async-start | bytes 442368 | tf_op jit(solution)/shard_map/reduce_scatter | solution.py:240
  469.4 122.3 %reduce-scatter.28.cloned.1.call-start = ((), (), s32[]{:S(2)}) async-start(), calls=%async_computation.16 | async-start | bytes 884736
  (62 other events, 214.3 us)
Sparse Core Ops, SparseCore 0:
  17.8 47.6 all-gather.1
  194.7 58.1 reduce-scatter.19
  255.1 42.3 reduce-scatter.15
  300.3 10.9 reduce-scatter.29
  315.4 75.5 reduce-scatter.25
  394.7 74.5 reduce-scatter.21
  473.7 67.0 reduce-scatter.17
  543.2 12.3 reduce-scatter.31
  557.8 11.9 reduce-scatter.23
  571.9 15.7 reduce-scatter.27
where the time goes:
time: 609 us; the launch traced here: 602 us
  waiting for transfers between devices  301 us (49%)
  matrix products  135 us (22%)
  local copies, waits for them, and re-layouts  57.3 us (9%)
  other arithmetic  50.4 us (8%)
  blocking collectives  41.5 us (7%)
  between operations  16 us (3%)
    reduce_scatter x1, waiting for transfers between devices, on_device(): lax.psum_scatter(matrices[3].astype(jnp.bfloat16), 'dp', scatter_dimensio...  76.8 us
    reduce_scatter x1, waiting for transfers between devices, on_device(): lax.psum_scatter(matrices[2].astype(jnp.bfloat16), 'dp', scatter_dimensio...  68.2 us
    reduce_scatter x1, waiting for transfers between devices, on_device(): lax.psum_scatter(matrices[0].astype(jnp.bfloat16), 'dp', scatter_dimensio...  59.9 us
    psum x1, blocking collectives, on_device(): lax.psum((gain_one_grad, bias_one_grad, query_bias_grad, value_bias_grad,...  41.5 us
    all_gather x1, waiting for transfers between devices, on_device(): shared_all = lax.all_gather(shared_local, 'tile', axis=1, tiled=True)  37.7 us
    reduce_scatter x1, waiting for transfers between devices, on_device(): lax.psum_scatter(matrices[1].astype(jnp.bfloat16), 'dp', scatter_dimensio...  32.2 us
    slice x15, local copies, waits for them, and re-layouts, split_heads(): sliced = source[..., column:column + head_block]  29.6 us
    unnamed x158, local copies, waits for them, and re-layouts  21.5 us
  transfers between devices with their start and end apart: 10, of which 7 were waited for; matrix products, arithmetic and copies ran while one was open for 16% of the time, Pallas kernels for 0%

commit v1 on v0

--- a/solution.py
+++ b/solution.py
@@ -1,9 +1,540 @@
 import jax
 import jax.numpy as jnp
 from jax import lax
+from jax.experimental import pallas as pl
+from jax.experimental.pallas import tpu as pltpu
 from jax.sharding import PartitionSpec as P
 
 HEAD_DIM = 64
+PAIR = 2 * HEAD_DIM
+MASKED = -1e30
+MESH = pl.DeviceIdType.MESH
+BF = jnp.bfloat16
+F32 = jnp.float32
+NT = (((1,), (1,)), ((), ()))
+TN = (((0,), (0,)), ((), ()))
+
+
+def mm(a, b):
+    return jnp.dot(a, b, preferred_element_type=F32)
+
+
+def mm_nt(a, b):
+    return lax.dot_general(a, b, NT, preferred_element_type=F32)
+
+
+def mm_tn(a, b):
+    return lax.dot_general(a, b, TN, preferred_element_type=F32)
+
+
+def any_spec():
+    return pl.BlockSpec(memory_space=pl.ANY)
+
+
+def vmem_spec():
+    return pl.BlockSpec(memory_space=pltpu.VMEM)
+
+
+def attention_forward(
+    tok, info, gain, bias, w_hbm, pbias, proj_out, norm_out, att_out, lse_out,
+    x, w, proj, norm, att, lse, mask, sems, send_sem, recv_sem,
+):
+    rows, width = norm.shape
+    half = rows // 2
+    heads = width // HEAD_DIM
+    t = lax.axis_index("tile")
+    far, near = t * half, (1 - t) * half
+    barrier = pltpu.get_barrier_semaphore()
+    pl.semaphore_signal(barrier, inc=1, device_id={"tile": 1 - t}, device_id_type=MESH)
+    load_far = pltpu.make_async_copy(tok.at[pl.ds(far, half)], x.at[pl.ds(0, half)], sems.at[0])
+    load_near = pltpu.make_async_copy(tok.at[pl.ds(near, half)], x.at[pl.ds(half, half)], sems.at[1])
+    load_w = pltpu.make_async_copy(w_hbm, w, sems.at[2])
+    load_far.start()
+    load_near.start()
+    load_w.start()
+    pl.semaphore_wait(barrier, 1)
+    halo = pltpu.make_async_remote_copy(
+        tok.at[pl.ds(near, half)], x.at[pl.ds(rows, half)], send_sem, recv_sem,
+        device_id={"tile": 1 - t}, device_id_type=MESH,
+    )
+    halo.start()
+
+    seg_row = info[1:2, :]
+    seg_col = jnp.transpose(info[...].astype(F32))[:, 0:1].astype(jnp.int32)
+    key_at = lax.broadcasted_iota(jnp.int32, (half, rows + half), 1)
+    for part in range(2):
+        query_at = lax.broadcasted_iota(jnp.int32, (half, rows + half), 0) + part * half
+        same = seg_col[part * half : (part + 1) * half] == seg_row
+        mask[pl.ds(part * half, half), :] = jnp.where(same | (query_at == key_at), 0.0, MASKED)
+
+    def normalize(start, count):
+        step = 128
+
+        def one(i, _):
+            at = pl.ds(pl.multiple_of(start + i * step, step), step)
+            v = x[at, :].astype(F32)
+            centred = v - jnp.mean(v, axis=-1, keepdims=True)
+            var = jnp.mean(centred * centred, axis=-1, keepdims=True)
+            norm_at = centred * lax.rsqrt(var + 1e-06) * gain[...] + bias[...]
+            x[at, :] = norm_at.astype(BF)
+            return 0
+
+        lax.fori_loop(0, count // step, one, 0)
+
+    def project(start, count):
+        cols = 768
+
+        def one(i, _):
+            at = pl.ds(pl.multiple_of(i * cols, cols), cols)
+            block = mm(x[pl.ds(start, count), :], w[:, at]) + pbias[:, at]
+            low = block.astype(BF)
+            scale = jnp.where(i * cols < width, HEAD_DIM ** (-0.5), 1.0).astype(BF)
+            proj[pl.ds(start, count), at] = low * scale
+            return 0
+
+        lax.fori_loop(0, 3 * width // cols, one, 0)
+
+    lane = lax.broadcasted_iota(jnp.int32, (1, PAIR), 1)
+    low_half = lane < HEAD_DIM
+
+    def attend(start, keys):
+        def one(p, _):
+            at = pl.multiple_of(p * PAIR, PAIR)
+            q = proj[pl.ds(start, half), pl.ds(at, PAIR)]
+            k = proj[pl.ds(0, keys), pl.ds(width + at, PAIR)]
+            v = proj[pl.ds(0, keys), pl.ds(2 * width + at, PAIR)]
+            total = None
+            tops = []
+            for head in range(2):
+                mine = low_half if head == 0 else ~low_half
+                qh = jnp.where(mine, q, 0).astype(BF)
+                s = mm_nt(qh, k) + mask[pl.ds(start, half), pl.ds(0, keys)]
+                top = jnp.max(s, axis=-1, keepdims=True)
+                e = jnp.exp(s - top).astype(BF)
+                ones = jnp.broadcast_to(jnp.where(mine, 1.0, 0.0).astype(BF), (keys, PAIR))
+                vh = jnp.concatenate([jnp.where(mine, v, 0).astype(BF), ones], axis=1)
+                part = mm(e, vh)
+                total = part if total is None else total + part
+                tops.append(top)
+            sums = total[:, PAIR:]
+            att[pl.ds(start, half), pl.ds(at, PAIR)] = (total[:, :PAIR] / sums).astype(BF)
+            logs = jnp.log(sums)
+            lane_of = lax.broadcasted_iota(jnp.int32, (half, PAIR), 1)
+            acc = lse[pl.ds(start, half), :]
+            acc = jnp.where(lane_of == 2 * p, tops[0] + logs[:, 0:1], acc)
+            acc = jnp.where(lane_of == 2 * p + 1, tops[1] + logs[:, HEAD_DIM : HEAD_DIM + 1], acc)
+            lse[pl.ds(start, half), :] = acc
+            return 0
+
+        lax.fori_loop(0, heads // 2, one, 0, unroll=6)
+
+    lse[...] = jnp.zeros_like(lse)
+    load_far.wait()
+    load_near.wait()
+    normalize(0, rows)
+    norm_copy = pltpu.make_async_copy(x.at[pl.ds(0, rows)], norm_out, sems.at[0])
+    norm_copy.start()
+    load_w.wait()
+    project(0, rows)
+    attend(0, rows)
+    halo.wait()
+    normalize(rows, half)
+    project(rows, half)
+    proj_copy = pltpu.make_async_copy(proj, proj_out, sems.at[1])
+    proj_copy.start()
+    attend(half, rows + half)
+    att_copy = pltpu.make_async_copy(att, att_out, sems.at[2])
+    att_copy.start()
+    lse_out[...] = jnp.transpose(lse[...])[:16, :]
+    norm_copy.wait()
+    proj_copy.wait()
+    att_copy.wait()
+
+
+def call_forward(tokens, info, gain, bias, w, pbias):
+    rows, width = tokens.shape
+    half = rows // 2
+    sds = jax.ShapeDtypeStruct
+    return pl.pallas_call(
+        attention_forward,
+        out_shape=(
+            sds((rows + half, 3 * width), BF),
+            sds((rows, width), BF),
+            sds((rows, width), BF),
+            sds((16, rows), F32),
+        ),
+        in_specs=[any_spec(), vmem_spec(), vmem_spec(), vmem_spec(), any_spec(), vmem_spec()],
+        out_specs=(any_spec(), any_spec(), any_spec(), vmem_spec()),
+        scratch_shapes=[
+            pltpu.VMEM((rows + half, width), BF),
+            pltpu.VMEM((width, 3 * width), BF),
+            pltpu.VMEM((rows + half, 3 * width), BF),
+            pltpu.VMEM((rows, width), BF),
+            pltpu.VMEM((rows, width), BF),
+            pltpu.VMEM((rows, PAIR), F32),
+            pltpu.VMEM((rows, rows + half), F32),
+            pltpu.SemaphoreType.DMA((3,)),
+            pltpu.SemaphoreType.DMA,
+            pltpu.SemaphoreType.DMA,
+        ],
+        compiler_params=pltpu.CompilerParams(collective_id=0, has_side_effects=True, vmem_limit_bytes=60 << 20),
+        name="attention_forward",
+    )(tokens, info, gain, bias, w, pbias)
+
+
+def gelu_and_slope(z):
+    bell = jnp.exp(z * z * -0.5)
+    t = 1.0 / (1.0 + jnp.abs(z) * (0.3275911 * 0.7071067811865476))
+    tail = t * (0.127414796 + t * (-0.142248368 + t * (0.7107068705 + t * (-0.7265760135 + t * 0.5307027145)))) * bell
+    upper = jnp.where(z >= 0, 1.0 - tail, tail)
+    return z * upper, upper + z * bell * 0.3989422804014327
+
+
+def mlp(
+    tok, att_hbm, dy_hbm, keep_col, ow_hbm, ob, g2, b2, w1_hbm, b1, w2_hbm, c2,
+    out_hbm, dh_hbm, db_hbm, da_hbm, delta_out, f1_hbm, f2_hbm, vec_out, b1g_out,
+    x, att, dy, ow, w1, w2, hidden, xhat, rstd, n2, n2t, z, da, act, di, acc, dn, f1, f2, obuf, sems,
+):
+    rows, width = hidden.shape
+    half = rows // 2
+    chunks, _, cols = w1.shape
+    t = lax.axis_index("tile")
+    far, near = t * half, (1 - t) * half
+    copies = []
+
+    def fetch(src, dst, i):
+        c = pltpu.make_async_copy(src, dst, sems.at[i])
+        c.start()
+        return c
+
+    got_att = fetch(att_hbm, att, 0)
+    got_ow = fetch(ow_hbm, ow, 1)
+    got_x = [fetch(tok.at[pl.ds(far, half)], x.at[pl.ds(0, half)], 2), fetch(tok.at[pl.ds(near, half)], x.at[pl.ds(half, half)], 3)]
+    got_dy = [fetch(dy_hbm.at[pl.ds(far, half)], dy.at[pl.ds(0, half)], 4), fetch(dy_hbm.at[pl.ds(near, half)], dy.at[pl.ds(half, half)], 5)]
+    got_w = []
+    for c in range(chunks):
+        got_w.append(fetch(w1_hbm.at[:, pl.ds(c * cols, cols)], w1.at[c], 6 + c))
+        got_w.append(fetch(w2_hbm.at[pl.ds(c * cols, cols)], w2.at[c], 6 + chunks + c))
+    got_att.wait()
+    got_ow.wait()
+    for g in got_x:
+        g.wait()
+    rb = 128
+    vec_out[...] = jnp.zeros_like(vec_out)
+
+    def add_vec(i, v):
+        vec_out[i : i + 1, :] += jnp.sum(v, axis=0, keepdims=True)
+
+    def front(i, _):
+        at = pl.ds(pl.multiple_of(i * rb, rb), rb)
+        branch = mm(att[at, :], ow[...]) + ob[...]
+        xs = x[at, :].astype(F32)
+        h = xs + branch
+        hidden[at, :] = h
+        kept = keep_col[at, :][:, 0:1]
+        add_vec(0, kept * xs * xs)
+        add_vec(1, kept * branch * branch)
+        centred = h - jnp.mean(h, axis=-1, keepdims=True)
+        r = lax.rsqrt(jnp.mean(centred * centred, axis=-1, keepdims=True) + 1e-06)
+        xh = centred * r
+        xhat[at, :] = xh
+        rstd[at, :] = jnp.broadcast_to(r, (rb, 128))
+        n2[at, :] = (xh * g2[...] + b2[...]).astype(BF)
+        return 0
+
+    lax.fori_loop(0, rows // rb, front, 0)
+    n2t[...] = jnp.transpose(n2[...])
+    acc[...] = jnp.zeros_like(acc)
+    dn[...] = jnp.zeros_like(dn)
+    for g in got_dy:
+        g.wait()
+    for c in range(2 * chunks):
+        got_w[c].wait()
+
+    def chunk(c, _):
+        w1c, w2c = w1.at[c], w2.at[c]
+        z[...] = mm(n2[...], w1c[...]) + b1[c]
+        da[...] = mm_nt(dy[...], w2c[...])
+        gr = 64
+        bsum = jnp.zeros((1, cols), F32)
+        for i in range(rows // gr):
+            at = pl.ds(i * gr, gr)
+            a, s = gelu_and_slope(z[at, :])
+            act[at, :] = a.astype(BF)
+            d = (da[at, :] * s).astype(BF)
+            di[at, :] = d
+            bsum = bsum + jnp.sum(d.astype(F32), axis=0, keepdims=True)
+        b1g_out[c] = bsum
+        acc[...] += mm(act[...], w2c[...])
+        dn[...] += mm_nt(di[...], w1c[...])
+        f1[c] = mm(n2t[...], di[...]).astype(BF)
+        f2[c] = mm_tn(act[...], dy[...]).astype(BF)
+        return 0
+
+    lax.fori_loop(0, chunks, chunk, 0, unroll=1)
+
+    def back(i, _):
+        at = pl.ds(pl.multiple_of(i * rb, rb), rb)
+        branch = acc[at, :] + c2[...]
+        result = hidden[at, :] + branch
+        obuf[at, :] = result.astype(BF)
+        kept = keep_col[at, :][:, 0:1]
+        add_vec(2, kept * branch * branch)
+        add_vec(3, kept * result * result)
+        g = dn[at, :]
+        xh = xhat[at, :]
+        add_vec(4, g * xh)
+        add_vec(5, g)
+        gy = g * g2[...]
+        mean_gy = jnp.mean(gy, axis=-1, keepdims=True)
+        mean_gx = jnp.mean(gy * xh, axis=-1, keepdims=True)
+        dys = dy[at, :].astype(F32)
+        add_vec(7, dys)
+        dh = dys + rstd[at, :][:, 0:1] * (gy - mean_gy - xh * mean_gx)
+        hidden[at, :] = dh
+        low = dh.astype(BF)
+        n2[at, :] = low
+        add_vec(6, low.astype(F32))
+        return 0
+
+    lax.fori_loop(0, rows // rb, back, 0)
+    copies.append(fetch(obuf.at[pl.ds(0, half)], out_hbm.at[pl.ds(far, half)], 0))
+    copies.append(fetch(obuf.at[pl.ds(half, half)], out_hbm.at[pl.ds(near, half)], 1))
+    copies.append(fetch(hidden, dh_hbm, 2))
+    copies.append(fetch(n2, db_hbm, 3))
+    copies.append(fetch(f1, f1_hbm, 4))
+    copies.append(fetch(f2, f2_hbm, 5))
+    d_att = mm_nt(n2[...], ow[...])
+    x[...] = d_att.astype(BF)
+    copies.append(fetch(x, da_hbm, 6))
+    heads = width // HEAD_DIM
+    head_of = lax.broadcasted_iota(jnp.int32, (16, width), 1) // HEAD_DIM
+    mine = (head_of == lax.broadcasted_iota(jnp.int32, (16, width), 0)).astype(F32).astype(BF)
+    prod = x[...].astype(F32) * att[...].astype(F32)
+    hi = prod.astype(BF)
+    lo = (prod - hi.astype(F32)).astype(BF)
+    delta_out[...] = mm_nt(mine, hi) + mm_nt(mine, lo)
+    for c in copies:
+        c.wait()
+
+
+def call_mlp(tokens, att, dy, keep_col, ow, ob, g2, b2, w1, b1, w2, c2):
+    rows, width = tokens.shape
+    hid = w1.shape[1]
+    cols = width
+    chunks = hid // cols
+    sds = jax.ShapeDtypeStruct
+    V = pltpu.VMEM
+    return pl.pallas_call(
+        mlp,
+        out_shape=(
+            sds((rows, width), BF), sds((rows, width), F32), sds((rows, width), BF), sds((rows, width), BF),
+            sds((16, rows), F32), sds((chunks, width, cols), BF), sds((chunks, cols, width), BF),
+            sds((8, width), F32), sds((chunks, 1, cols), F32),
+        ),
+        in_specs=[any_spec(), any_spec(), any_spec(), vmem_spec(), any_spec(), vmem_spec(), vmem_spec(), vmem_spec(), any_spec(), vmem_spec(), any_spec(), vmem_spec()],
+        out_specs=(any_spec(),) * 4 + (vmem_spec(), any_spec(), any_spec(), vmem_spec(), vmem_spec()),
+        scratch_shapes=[
+            V((rows, width), BF), V((rows, width), BF), V((rows, width), BF), V((width, width), BF),
+            V((chunks, width, cols), BF), V((chunks, cols, width), BF),
+            V((rows, width), F32), V((rows, width), F32), V((rows, 128), F32), V((rows, width), BF), V((width, rows), BF),
+            V((rows, cols), F32), V((rows, cols), F32), V((rows, cols), BF), V((rows, cols), BF),
+            V((rows, width), F32), V((rows, width), F32), V((chunks, width, cols), BF), V((chunks, cols, width), BF),
+            V((rows, width), BF),
+            pltpu.SemaphoreType.DMA((6 + 2 * chunks,)),
+        ],
+        compiler_params=pltpu.CompilerParams(vmem_limit_bytes=62 << 20),
+        name="feed_forward",
+    )(tokens, att, dy, keep_col, ow, ob, g2, b2, w1, b1.reshape(chunks, 1, cols), w2, c2)
+
+
+def attention_backward(
+    tok, info, gain, proj_hbm, norm_hbm, att_hbm, dh_hbm, db_hbm, da_hbm, lse, delta, w_hbm,
+    gt_hbm, qg_hbm, og_hbm, vec_out,
+    x, proj, norm, att, dh, db, da, w, normt, attt, stat, mask, near_key, near_query, dk, dv, dproj, dn, qg, og, obuf, sems, send_sems, recv_sems,
+):
+    rows, width = norm.shape
+    half = rows // 2
+    heads = width // HEAD_DIM
+    t = lax.axis_index("tile")
+    far, near = t * half, (1 - t) * half
+    barrier = pltpu.get_barrier_semaphore()
+    pl.semaphore_signal(barrier, inc=1, device_id={"tile": 1 - t}, device_id_type=MESH)
+
+    def fetch(src, dst, i):
+        c = pltpu.make_async_copy(src, dst, sems.at[i])
+        c.start()
+        return c
+
+    got_proj = fetch(proj_hbm, proj, 0)
+    got_da = fetch(da_hbm, da.at[pl.ds(0, rows)], 1)
+    got_att = fetch(att_hbm, att, 2)
+    got_db = fetch(db_hbm, db, 3)
+    got_norm = fetch(norm_hbm, norm, 4)
+    got_w = fetch(w_hbm, w, 5)
+    got_dh = fetch(dh_hbm, dh, 6)
+    got_x = [fetch(tok.at[pl.ds(far, half)], x.at[pl.ds(0, half)], 7), fetch(tok.at[pl.ds(near, half)], x.at[pl.ds(half, half)], 8)]
+    pl.semaphore_wait(barrier, 1)
+    halos = []
+    for i, (src, dst) in enumerate(
+        (
+            (da_hbm.at[pl.ds(half, half)], da.at[pl.ds(rows, half)]),
+            (lse.at[:, pl.ds(half, half)], stat.at[0]),
+            (delta.at[:, pl.ds(half, half)], stat.at[1]),
+        )
+    ):
+        h = pltpu.make_async_remote_copy(src, dst, send_sems.at[i], recv_sems.at[i], device_id={"tile": 1 - t}, device_id_type=MESH)
+        h.start()
+        halos.append(h)
+
+    seg_row = info[0:1, :]
+    key_col = jnp.transpose(info[...].astype(F32))[:, 1:2].astype(jnp.int32)
+    key_at = lax.broadcasted_iota(jnp.int32, (half, rows), 0)
+    query_at = lax.broadcasted_iota(jnp.int32, (half, rows), 1)
+    for part in range(2):
+        same = key_col[part * half : (part + 1) * half] == seg_row[:, :rows]
+        mask[pl.ds(part * half, half), :] = jnp.where(same | (query_at == key_at + part * half), 0.0, MASKED)
+    near_key[...] = jnp.where(key_col[half:rows] == seg_row[:, rows:], 0.0, MASKED)
+    near_query[...] = jnp.where(key_col[rows:] == seg_row[:, half:rows], 0.0, MASKED)
+    got_att.wait()
+    attt[...] = jnp.transpose(att[...])
+    got_db.wait()
+    og[...] = mm(attt[...], db[...]).astype(BF)
+    got_norm.wait()
+    normt[...] = jnp.transpose(norm[...])
+    got_proj.wait()
+    got_da.wait()
+
+    lane = lax.broadcasted_iota(jnp.int32, (1, PAIR), 1)
+
+    def cut(v, head):
+        return jnp.where((lane < HEAD_DIM) == (head == 0), v, 0).astype(BF)
+
+    def own(p, _):
+        at = pl.multiple_of(p * PAIR, PAIR)
+        col = pl.ds(at, PAIR)
+        kcol, vcol = pl.ds(width + at, PAIR), pl.ds(2 * width + at, PAIR)
+        q, k, v = proj[pl.ds(0, rows), col], proj[:, kcol], proj[:, vcol]
+        do = da[pl.ds(0, rows), col]
+        gq = gk = gv = gn = None
+        for head in range(2):
+            qh, kh, doh = cut(q, head), cut(k, head), cut(do, head)
+            ls = lse[pl.ds(2 * p + head, 1), :]
+            de = delta[pl.ds(2 * p + head, 1), :]
+            s = mm_nt(k[:rows], qh) + mask[...]
+            prob = jnp.exp(s - ls)
+            dp = mm_nt(v[:rows], doh)
+            ds = (prob * (dp - de)).astype(BF)
+            low = prob.astype(BF)
+            a = mm(low, doh)
+            b = mm(ds, qh)
+            c = mm_tn(ds, kh[:rows])
+            s2 = mm_nt(k[rows:], qh[half:]) + near_query[...]
+            prob2 = jnp.exp(s2 - ls[:, half:])
+            dp2 = mm_nt(v[rows:], doh[half:])
+            ds2 = (prob2 * (dp2 - de[:, half:])).astype(BF)
+            d = mm_tn(ds2, kh[rows:])
+            gv = a if gv is None else gv + a
+            gk = b if gk is None else gk + b
+            gq = c if gq is None else gq + c
+            gn = d if gn is None else gn + d
+        scale = HEAD_DIM ** (-0.5)
+        dproj[pl.ds(0, half), col] = (gq[:half] * scale).astype(BF)
+        dproj[pl.ds(half, half), col] = ((gq[half:] + gn) * scale).astype(BF)
+        dproj[pl.ds(0, half), kcol] = gk[:half].astype(BF)
+        dproj[pl.ds(0, half), vcol] = gv[:half].astype(BF)
+        dk[:, col] = gk[half:]
+        dv[:, col] = gv[half:]
+        return 0
+
+    def halo(p, _):
+        at = pl.multiple_of(p * PAIR, PAIR)
+        col = pl.ds(at, PAIR)
+        kcol, vcol = pl.ds(width + at, PAIR), pl.ds(2 * width + at, PAIR)
+        q, k, v = proj[pl.ds(rows, half), col], proj[pl.ds(half, half), kcol], proj[pl.ds(half, half), vcol]
+        do = da[pl.ds(rows, half), col]
+        gk, gv = dk[:, col], dv[:, col]
+        for head in range(2):
+            qh, doh = cut(q, head), cut(do, head)
+            ls = stat[0, pl.ds(2 * p + head, 1), :]
+            de = stat[1, pl.ds(2 * p + head, 1), :]
+            prob = jnp.exp(mm_nt(k, qh) + near_key[...] - ls)
+            ds = (prob * (mm_nt(v, doh) - de)).astype(BF)
+            gv = gv + mm(prob.astype(BF), doh)
+            gk = gk + mm(ds, qh)
+        dproj[pl.ds(half, half), kcol] = gk.astype(BF)
+        dproj[pl.ds(half, half), vcol] = gv.astype(BF)
+        return 0
+
+    lax.fori_loop(0, heads // 2, own, 0, unroll=6)
+    for h in halos:
+        h.wait()
+    lax.fori_loop(0, heads // 2, halo, 0, unroll=6)
+    got_w.wait()
+    got_dh.wait()
+    for g in got_x:
+        g.wait()
+    vec_out[...] = jnp.zeros_like(vec_out)
+
+    def add_vec(i, v):
+        vec_out[i : i + 1, :] += jnp.sum(v, axis=0, keepdims=True)
+
+    for j in range(3):
+        cols = pl.ds(j * width, width)
+        qg[j] = mm(normt[...], dproj[:, cols]).astype(BF)
+    dn[...] = mm_nt(dproj[...], w[...])
+    rb = 128
+
+    def back(i, _):
+        at = pl.ds(pl.multiple_of(i * rb, rb), rb)
+        xs = x[at, :].astype(F32)
+        centred = xs - jnp.mean(xs, axis=-1, keepdims=True)
+        r = lax.rsqrt(jnp.mean(centred * centred, axis=-1, keepdims=True) + 1e-06)
+        xh = centred * r
+        g = dn[at, :]
+        add_vec(0, g * xh)
+        add_vec(1, g)
+        gy = g * gain[...]
+        mean_gy = jnp.mean(gy, axis=-1, keepdims=True)
+        mean_gx = jnp.mean(gy * xh, axis=-1, keepdims=True)
+        obuf[at, :] = (dh[at, :] + r * (gy - mean_gy - xh * mean_gx)).astype(BF)
+        add_vec(2, dproj[at, pl.ds(0, width)].astype(F32))
+        add_vec(3, dproj[at, pl.ds(2 * width, width)].astype(F32))
+        return 0
+
+    lax.fori_loop(0, rows // rb, back, 0)
+    copies = [
+        fetch(obuf.at[pl.ds(0, half)], gt_hbm.at[pl.ds(far, half)], 0),
+        fetch(obuf.at[pl.ds(half, half)], gt_hbm.at[pl.ds(near, half)], 1),
+        fetch(qg, qg_hbm, 2),
+        fetch(og, og_hbm, 3),
+    ]
+    for c in copies:
+        c.wait()
+
+
+def call_backward(tokens, info, gain, proj, norm, att, dh, db, da, lse, delta, w):
+    rows, width = tokens.shape
+    half = rows // 2
+    sds = jax.ShapeDtypeStruct
+    V = pltpu.VMEM
+    return pl.pallas_call(
+        attention_backward,
+        out_shape=(sds((rows, width), BF), sds((3, width, width), BF), sds((width, width), BF), sds((8, width), F32)),
+        in_specs=[any_spec(), vmem_spec(), vmem_spec()] + [any_spec()] * 6 + [vmem_spec(), vmem_spec(), any_spec()],
+        out_specs=(any_spec(),) * 3 + (vmem_spec(),),
+        scratch_shapes=[
+            V((rows, width), BF), V((rows + half, 3 * width), BF), V((rows, width), BF), V((rows, width), BF),
+            V((rows, width), F32), V((rows, width), BF), V((rows + half, width), BF), V((width, 3 * width), BF),
+            V((width, rows), BF), V((width, rows), BF), V((2, 16, half), F32),
+            V((rows, rows), F32), V((half, half), F32), V((half, half), F32),
+            V((half, width), F32), V((half, width), F32), V((rows, 3 * width), BF), V((rows, width), F32),
+            V((3, width, width), BF), V((width, width), BF), V((rows, width), BF),
+            pltpu.SemaphoreType.DMA((9,)), pltpu.SemaphoreType.DMA((3,)), pltpu.SemaphoreType.DMA((3,)),
+        ],
+        compiler_params=pltpu.CompilerParams(collective_id=1, has_side_effects=True, vmem_limit_bytes=62 << 20),
+        name="attention_backward",
+    )(tokens, info, gain, proj, norm, att, dh, db, da, lse, delta, w)
 
 
 def layer_norm(values, norm_gain, norm_bias):
@@ -17,7 +548,7 @@
     return jax.nn.gelu(values, approximate=False)
 
 
-def on_device(
+def on_device_general(
     tokens,
     segment_ids,
     keep_mask,
@@ -266,47 +797,35 @@
     )
 
 
+def on_device(tokens,segment_ids,keep_mask,gain_one,bias_one,qkv_weight,query_bias,value_bias,out_weight,out_bias,gain_two,bias_two,fc1_weight,fc1_bias,fc2_weight,fc2_bias,cotangent):
+    _,rows,width=tokens.shape; half=rows//2
+    t=lax.axis_index("tile"); base=t*rows
+    ofs=(base+t*half,base+(1-t)*half,(1-t)*rows+t*half)
+    def order(v): return jnp.concatenate([lax.dynamic_slice_in_dim(v,o,half,0) for o in ofs])
+    s=order(segment_ids[0]); k=order(keep_mask[0])
+    info=jnp.concatenate([jnp.stack([s,jnp.where(k==1,s,-1)]),jnp.zeros((6,s.shape[0]),jnp.int32)])
+    row=lambda v:v[None]
+    pb=jnp.concatenate([query_bias,jnp.zeros_like(query_bias),value_bias])[None]
+    proj,norm,att,lse=call_forward(tokens[0],info,row(gain_one),row(bias_one),qkv_weight,pb)
+    kc=jnp.broadcast_to(k[:rows,None].astype(jnp.float32),(rows,128))
+    out,dh,db,da,delta,f1,f2,vec,b1g=call_mlp(tokens[0],att,cotangent[0],kc,out_weight,row(out_bias),row(gain_two),row(bias_two),fc1_weight,fc1_bias,fc2_weight,row(fc2_bias))
+    gt,qg,og,vec2=call_backward(tokens[0],info,row(gain_one),proj,norm,att,dh,db,da,lse,delta,qkv_weight)
+    stats=jnp.concatenate([vec[:4].sum(1),k[:rows].astype(jnp.float32).sum()[None]])
+    small=lax.psum((vec2[0],vec2[1],vec2[2],vec2[3],vec[6],vec[4],vec[5],b1g.reshape(-1),vec[7],stats),("dp","tile"))
+    mats=(qg.swapaxes(0,1).reshape(width,3*width),og,f1.swapaxes(0,1).reshape(width,-1),f2.reshape(-1,width))
+    red=[]
+    for m in mats:
+        m=lax.psum_scatter(m,"dp",scatter_dimension=0,tiled=True)
+        red.append(lax.psum_scatter(m,"tile",scatter_dimension=1,tiled=True).astype(jnp.float32))
+    tot=small[9]
+    rm=jnp.sqrt(tot[:4]/(tot[4]*width))
+    return (out[None],gt[None],small[0],small[1],red[0],small[2],small[3],red[1],small[4],small[5],small[6],red[2],small[7],red[3],small[8],rm)
+def fits(mesh):
+    return mesh.shape["tile"] == 2 and mesh.shape["dp"] == 16
+
+
 def solution(mesh):
-    placed = (
-        P("dp", "tile", None),
-        P("dp", None),
-        P("dp", None),
-        P(),
-        P(),
-        P(),
-        P(),
-        P(),
-        P(),
-        P(),
-        P(),
-        P(),
-        P(),
-        P(),
-        P(),
-        P(),
-        P("dp", "tile", None),
-    )
-    return jax.shard_map(
-        on_device,
-        mesh=mesh,
-        in_specs=placed,
-        out_specs=(
-            P("dp", "tile", None),
-            P("dp", "tile", None),
-            P(),
-            P(),
-            P("dp", "tile"),
-            P(),
-            P(),
-            P("dp", "tile"),
-            P(),
-            P(),
-            P(),
-            P("dp", "tile"),
-            P(),
-            P("dp", "tile"),
-            P(),
-            P(),
-        ),
-        check_vma=False,
-    )
+    S=P("dp","tile",None); D=P("dp",None)
+    placed=(S,D,D)+(P(),)*13+(S,)
+    T=P("dp","tile")
+    return jax.shard_map(on_device if fits(mesh) else on_device_general,mesh=mesh,in_specs=placed,out_specs=(S,S,P(),P(),T,P(),P(),T,P(),P(),P(),T,P(),T,P(),P()),check_vma=False)

time: 609 us -> 480 us (0.79)
  matrix products: 135 us -> 0 us
  Pallas kernels: 0 us -> 87.9 us
  other arithmetic: 50.4 us -> 4.77 us
  waiting for transfers between devices: 301 us -> 275 us
  local copies, waits for them, and re-layouts: 57.3 us -> 46.5 us
    unnamed x13 -> x12, waiting for transfers between devices: 7.82 us -> 147 us
    dot_general x30 -> x0, matrix products: 135 us -> none  [the longest x3 21.2 us: on_device(): jnp.einsum('sqhe,skhe->shqk', grad_part, value_part, preferred_element_ty...]
    reduce_scatter x6 -> x4, waiting for transfers between devices: 256 us -> 128 us  [the longest x2 113 us: on_device(): m = lax.psum_scatter(m, 'dp', scatter_dimension=0, tiled=True)]
    pallas_call x0 -> x3, Pallas kernels: none -> 87.9 us  [the longest x1 35.7 us: call_backward(): pl.pallas_call(attention_backward, out_shape=(sds((rows, width), BF), sds...]
    all_gather x1 -> x0, waiting for transfers between devices: 37.7 us -> none  [on_device(): shared_all = lax.all_gather(shared_local, 'tile', axis=1, tiled=True)]
    slice x18 -> x3, local copies, waits for them, and re-layouts: 32.1 us -> 0.65 us  [the longest x1 0.58 us: on_device(): rm = jnp.sqrt(tot[:4] / (tot[4] * width))]
    convert_element_type x7 -> x3, other arithmetic: 22.6 us -> 1.39 us  [the longest x2 1.39 us: on_device(): lax.psum_scatter(m, 'tile', scatter_dimension=1, tiled=True)]
    reduce_sum x12 -> x2, other arithmetic: 19.9 us -> 0.72 us  [the longest x1 0.61 us: on_device(): k[:rows].astype(jnp.float32).sum()[None]]
  transfers between devices with their start and end apart: 10 -> 8, of which waited for: 7 -> 5; matrix products, arithmetic and copies ran while one was open for 16% -> 8% of each run, Pallas kernels for 0% -> 0%
where the time goes in v1:
time: 480 us; the launch traced here: 471 us
  waiting for transfers between devices  275 us (57%)
  Pallas kernels  87.9 us (18%)
  local copies, waits for them, and re-layouts  46.5 us (10%)
  blocking collectives  40.9 us (9%)
  between operations  15.1 us (3%)
    unnamed x12, waiting for transfers between devices  147 us
    reduce_scatter x2, waiting for transfers between devices, on_device(): m = lax.psum_scatter(m, 'dp', scatter_dimension=0, tiled=True)  113 us
    psum x1, blocking collectives, on_device(): lax.psum((vec2[0], vec2[1], vec2[2], vec2[3], vec[6], vec[4], vec[5], b1g...  40.9 us
    pallas_call x1, Pallas kernels, call_backward(): pl.pallas_call(attention_backward, out_shape=(sds((rows, width), BF), sds...  35.7 us
    pallas_call x1, Pallas kernels, call_mlp(): pl.pallas_call(mlp, out_shape=(sds((rows, width), BF), sds((rows, width),...  31.9 us
    unnamed x19, local copies, waits for them, and re-layouts  25 us
    pallas_call x1, Pallas kernels, call_forward(): pl.pallas_call(attention_forward, out_shape=(sds((rows + half, 3 * width)...  20.2 us
    reduce_scatter x2, waiting for transfers between devices, on_device(): lax.psum_scatter(m, 'tile', scatter_dimension=1, tiled=True)  14.9 us
  transfers between devices with their start and end apart: 8, of which 5 were waited for; matrix products, arithmetic and copies ran while one was open for 8% of the time, Pallas kernels for 0%

profile of v1, /device:TPU:0, one launch (start us, length us, event | category | flops | bytes accessed | tf_op | source)
XLA Modules:
  0.0 470.6 jit_solution(18203046014574438953)
XLA Ops:
  7.3 1.3 broadcast_in_dim.49.gain
  8.6 1.3 broadcast_in_dim.50.bias
  9.9 1.3 broadcast_in_dim.54.ob
  11.1 1.3 broadcast_in_dim.55.g2
  12.4 1.3 broadcast_in_dim.56.b2
  17.7 20.2 %attention_forward.1 = (bf16[768,2304]{1,0:T(8,128)(2,1)}, bf16[512,768]{1,0:T(8,128)(2,1)}, bf16[512,768]{1,0:T(8,128)(2,1)}, f32[16,512]{1,0:T(8,128)}) custom-call(bf16[512,768]{1,0:T(8,128)(2,1)} %bitcast.26, s32[8,768]{1,0:T(8,128)} %add_add_fusion.info, f32[1,768]{1,0:T(1,128)} %broadcast_in_dim.49.gain, f32[1,768]{1,0:T(1,128)} %broadcast_in_dim.50.bias, ...), custom_call_target="tpu_custom_call" | custom-call | tf_op jit(solution)/shard_map/attention_forward/pallas_call | solution.py:158
  38.8 31.9 %feed_forward.1 = (bf16[512,768]{1,0:T(8,128)(2,1)}, f32[512,768]{1,0:T(8,128)}, bf16[512,768]{1,0:T(8,128)(2,1)}, bf16[512,768]{1,0:T(8,128)(2,1)}, f32[16,512]...) custom-call(bf16[512,768]{1,0:T(8,128)(2,1)} %bitcast.27, ...), custom_call_target="tpu_custom_call" | custom-call | tf_op jit(solution)/shard_map/feed_forward/pallas_call | solution.py:328
  70.7 35.7 %attention_backward.1 = (bf16[512,768]{1,0:T(8,128)(2,1)}, bf16[3,768,768]{2,1,0:T(8,128)(2,1)}, bf16[768,768]{1,0:T(8,128)(2,1)}, f32[8,768]{1,0:T(8,128)}) custom-call(bf16[512,768]{1,0:T(8,128)(2,1)} %bitcast.28, s32[8,768]{1,0:T(8,128)} %add_add_fusion.info, f32[1,768]{1,0:T(1,128)} %broadcast_in_dim.49.gain, ...), custom_call_target="tpu_custom_call" | custom-call | tf_op jit(solution)/shard_map/attention_backward/pallas_call | solution.py:521
  106.5 4.3 copy.37
  110.8 4.0 copy.41
  115.6 6.7 %copy.38 = bf16[768,4,768]{0,2,1:T(8,128)(2,1)} copy(bf16[768,4,768]{2,0,1:T(8,128)(2,1)} %bitcast.30) | data formatting | bytes 9437184 | tf_op jit(solution)/shard_map/transpose | solution.py:815
  122.3 6.7 %copy.45 = bf16[768,3072]{1,0:T(8,128)(2,1)} copy(bf16[768,3072]{0,1:T(8,128)(2,1)} %bitcast.24) | data formatting | bytes 9437184
  129.2 37.0 %reduce-scatter.19.cloned.1.call-done = bf16[48,768]{1,0:T(8,128)(2,1)} async-done(((bf16[768,768]{1,0:T(8,128)(2,1)}), bf16[48,768]{1,0:T(8,128)(2,1)}) %reduce-scatter.19.cloned.1.call-update) | async-done | bytes 73744 | tf_op jit(solution)/shard_map/reduce_scatter | solution.py:818
  166.2 1.7 copy.43
  167.9 69.2 %reduce-scatter.25.cloned.1.call-done = bf16[48,2304]{1,0:T(8,128)(2,1)} async-done(((bf16[768,2304]{1,0:T(8,128)(2,1)}), bf16[48,2304]{1,0:T(8,128)(2,1)}) %reduce-scatter.25.cloned.1.call-update) | async-done | bytes 221200
  237.2 2.0 copy.42
  239.2 76.3 %reduce-scatter.23.cloned.1.call-done = bf16[192,768]{1,0:T(8,128)(2,1)} async-done(((bf16[3072,768]{1,0:T(8,128)(2,1)}), bf16[192,768]{1,0:T(8,128)(2,1)}) %reduce-scatter.23.cloned.1.call-update) | async-done | bytes 294928 | tf_op jit(solution)/shard_map/reduce_scatter | solution.py:818
  315.5 1.9 copy.47
  317.4 76.9 %reduce-scatter.29.cloned.1.call-done = bf16[48,3072]{1,0:T(8,128)(2,1)} async-done(((bf16[768,3072]{1,0:T(8,128)(2,1)}), bf16[48,3072]{1,0:T(8,128)(2,1)}) %reduce-scatter.29.cloned.1.call-update) | async-done | bytes 294928
  394.3 2.1 copy.46
  398.0 40.9 %all-reduce = (f32[768]{0:T(1024)}, f32[768]{0:T(1024)}, f32[768]{0:T(1024)}, f32[768]{0:T(1024)}, f32[768]{0:T(1024)}, /*index=5*/f32[768]{0:T(1024)}, f32[768]...) all-reduce(f32[768]{0:T(1024)S(1)} %get-tuple-element.89, ...), channel_id=1, replica_groups=mesh['dp'=16,'tile'=2] {'dp','tile'}, use_global_device_ids=true, to_apply=%region_0.1 | all-reduce | flops 9221 | bytes 73768 | tf_op jit(solution)/shard_map/psum | solution.py:814
  442.3 1.8 copy.39
  446.0 14.9 %reduce-scatter.21.cloned.1.call-done = bf16[48,1536]{0,1:T(8,128)(2,1)} async-done(((bf16[48,3072]{0,1:T(8,128)(2,1)}), bf16[48,1536]{0,1:T(8,128)(2,1)}) %reduce-scatter.21.cloned.1.call-update) | async-done | bytes 147472 | tf_op jit(solution)/shard_map/reduce_scatter | solution.py:819
  460.8 1.9 copy.40
  (52 shorter events, 13.0 us)
Async XLA Ops:
  7.2 159.0 %reduce-scatter.19.cloned.1.call-start = ((), (), s32[]{:S(2)}) async-start(), calls=%async_computation.9 | async-start | bytes 1253376 | tf_op jit(solution)/shard_map/reduce_scatter | solution.py:818
  106.5 130.7 %reduce-scatter.25.cloned.1.call-start = ((), (), s32[]{:S(2)}) async-start(), calls=%async_computation.12 | async-start | bytes 3760128
  114.9 200.6 %reduce-scatter.23.cloned.1.call-start = ((), (), s32[]{:S(2)}) async-start(), calls=%async_computation.11 | async-start | bytes 5013504 | tf_op jit(solution)/shard_map/reduce_scatter | solution.py:818
  115.6 278.8 %reduce-scatter.29.cloned.1.call-start = ((), (), s32[]{:S(2)}) async-start(), calls=%async_computation.14 | async-start | bytes 5013504
  129.1 267.4 %copy-start.1 = (f32[8,768]{1,0:T(8,128)S(1)}, f32[8,768]{1,0:T(8,128)}, u32[]{:S(2)}) copy-start(f32[8,768]{1,0:T(8,128)} %get-tuple-element.46) | copy-start | bytes 73732
  129.1 268.8 %copy-start.3 = (f32[8,768]{1,0:T(8,128)S(1)}, f32[8,768]{1,0:T(8,128)}, u32[]{:S(2)}) copy-start(f32[8,768]{1,0:T(8,128)} %get-tuple-element.43) | copy-start | bytes 73732
  129.1 268.9 %copy-start.2 = (f32[4,1,768]{2,1,0:T(1,128)S(1)}, f32[4,1,768]{2,1,0:T(1,128)}, u32[]{:S(2)}) copy-start(f32[4,1,768]{2,1,0:T(1,128)} %get-tuple-element.48) | copy-start | bytes 36868
  129.1 311.6 %reduce-scatter.27.cloned.1.call-start = ((), (), s32[]{:S(2)}) async-start(), calls=%async_computation.13 | async-start | bytes 294912
  167.9 294.8 %copy-start = (bf16[512,768]{1,0:T(8,128)(2,1)S(1)}, bf16[512,768]{1,0:T(8,128)(2,1)}, u32[]{:S(2)}) copy-start(bf16[512,768]{1,0:T(8,128)(2,1)} %get-tuple-element.42) | copy-start | bytes 2359300
  167.9 274.5 %reduce-scatter.17.cloned.1.call-start = ((), (), s32[]{:S(2)}) async-start(), calls=%async_computation.8 | async-start | bytes 884736 | tf_op jit(solution)/shard_map/reduce_scatter | solution.py:819
  239.2 205.0 %reduce-scatter.31.cloned.1.call-start = ((), (), s32[]{:S(2)}) async-start(), calls=%async_computation.15 | async-start | bytes 589824
  317.4 143.4 %reduce-scatter.21.cloned.1.call-start = ((), (), s32[]{:S(2)}) async-start(), calls=%async_computation.10 | async-start | bytes 1179648 | tf_op jit(solution)/shard_map/reduce_scatter | solution.py:819
Sparse Core Ops, SparseCore 0:
  106.6 59.5 reduce-scatter.18
  170.0 67.0 reduce-scatter.24
  241.0 74.4 reduce-scatter.22
  319.7 74.6 reduce-scatter.28
  397.0 10.3 reduce-scatter.26
  409.5 15.1 reduce-scatter.16
  427.1 13.5 reduce-scatter.30
  443.5 17.3 reduce-scatter.20

commit v2 on v0

--- a/solution.py
+++ b/solution.py
@@ -1,9 +1,749 @@
+import itertools
+
 import jax
 import jax.numpy as jnp
 from jax import lax
+from jax.experimental import pallas as pl
+from jax.experimental.pallas import tpu as pltpu
 from jax.sharding import PartitionSpec as P
 
 HEAD_DIM = 64
+PAIR = 2 * HEAD_DIM
+MASKED = -1e30
+MESH = pl.DeviceIdType.MESH
+BF = jnp.bfloat16
+F32 = jnp.float32
+NT = (((1,), (1,)), ((), ()))
+TN = (((0,), (0,)), ((), ()))
+
+
+def mm(a, b):
+    return jnp.dot(a, b, preferred_element_type=F32)
+
+
+def mm_nt(a, b):
+    return lax.dot_general(a, b, NT, preferred_element_type=F32)
+
+
+def mm_tn(a, b):
+    return lax.dot_general(a, b, TN, preferred_element_type=F32)
+
+
+def any_spec():
+    return pl.BlockSpec(memory_space=pl.ANY)
+
+
+def vmem_spec():
+    return pl.BlockSpec(memory_space=pltpu.VMEM)
+
+
+def gelu_and_slope(z):
+    bell = jnp.exp(z * z * -0.5)
+    t = 1.0 / (1.0 + jnp.abs(z) * (0.3275911 * 0.7071067811865476))
+    tail = t * (0.127414796 + t * (-0.142248368 + t * (0.7107068705 + t * (-0.7265760135 + t * 0.5307027145)))) * bell
+    upper = jnp.where(z >= 0, 1.0 - tail, tail)
+    return z * upper, upper + z * bell * 0.3989422804014327
+
+
+def place():
+    d = lax.axis_index("dp")
+    return dict(core=d % 2, y=d // 2 % 2, z0=d // 4 % 2, z1=d // 8, x=lax.axis_index("tile"))
+
+
+def peer(at, bit):
+    if bit == "x":
+        return {"tile": 1 - at["x"]}
+    step = dict(core=1, y=2, z0=4, z1=8)[bit]
+    return {"dp": lax.axis_index("dp") + step - 2 * step * at[bit]}
+
+
+def send(at, bit, src, dst, send_sem, recv_sem):
+    c = pltpu.make_async_remote_copy(src, dst, send_sem, recv_sem, device_id=peer(at, bit), device_id_type=MESH)
+    c.start()
+    return c
+
+
+class Share:
+    def __init__(self, at, ref, dims, order, buffers, send_sems, recv_sems, first):
+        self.at, self.ref, self.dims, self.buffers = at, ref, dims, list(buffers)
+        self.order, self.sems, self.next = list(order), (send_sems, recv_sems), first
+
+    def start(self):
+        bit = self.order.pop(0)
+        self.axis = self.dims.index(bit)
+        self.mine = self.at[bit]
+        lead = (slice(None),) * self.axis
+        self.other = self.buffers.pop(0)
+        i, self.next = self.next, self.next + 1
+        self.copy = send(self.at, bit, self.ref.at[lead + (1 - self.mine,)], self.other, self.sems[0].at[i], self.sems[1].at[i])
+
+    def kept(self, index):
+        return self.ref[index[: self.axis] + (self.mine,) + index[self.axis :]]
+
+    def finish(self):
+        self.copy.wait()
+        for index in itertools.product(*map(range, self.other.shape[:-2])):
+            self.other[index] = self.other[index] + self.kept(index)
+        self.ref = self.other
+        self.dims = self.dims[: self.axis] + self.dims[self.axis + 1 :]
+
+    def step(self):
+        self.finish()
+        self.start()
+
+    def last(self, put):
+        self.copy.wait()
+        for index in itertools.product(*map(range, self.other.shape[:-2])):
+            put(index, self.other[index].astype(F32) + self.kept(index).astype(F32))
+
+
+class Total:
+    def __init__(self, at, ref, buffers, send_sems, recv_sems, first):
+        self.at, self.ref, self.buffers = at, ref, buffers
+        self.sems, self.next, self.stage = (send_sems, recv_sems), first, 0
+
+    def start(self):
+        i = self.next + self.stage
+        self.copy = send(self.at, BITS[self.stage], self.ref, self.buffers.at[self.stage], self.sems[0].at[i], self.sems[1].at[i])
+
+    def finish(self):
+        self.copy.wait()
+        got = self.buffers.at[self.stage]
+        got[...] = self.ref[...] + got[...]
+        self.ref, self.stage = got, self.stage + 1
+
+    def step(self):
+        self.finish()
+        self.start()
+
+
+BITS = ("core", "y", "z0", "z1", "x")
+PART_A = (("z1", "z0", "y"), ("z0", "y", "z1"))
+PART_B = (("z1", "z0", "x"), ("x", "z0", "z1"))
+PART_C = (("x", "j", "z1", "z0"), ("z0", "x", "z1"))
+PART_D = (("x", "j", "z1", "y"), ("y", "x", "z1"))
+MATRIX = ("z1", "z0", "y", "core", "x")
+ORDERS = (("core", "x", "y", "z0", "z1"), ("core", "y", "z0", "x", "z1"), ("core", "z0", "x", "y", "z1"))
+OUT_ORDER = ("core", "y", "z0", "x", "z1")
+
+
+def stage_shapes(dims, order, rows, cols):
+    left, shapes = list(dims), []
+    for bit in order:
+        left.remove(bit)
+        shapes.append((2,) * len(left) + (rows, cols))
+    return shapes
+
+
+def everything(
+    tok, seg_hbm, keep_hbm, g1_hbm, bias1_hbm, wqkv_hbm, qb_hbm, vb_hbm, ow_hbm, ob_hbm, g2_hbm, bias2_hbm, w1_hbm, b1_hbm, w2_hbm, c2_hbm, dy_hbm,
+    out_hbm, gt_hbm, qkv_hbm, o_hbm, fc1_hbm, fc2_hbm, vec_hbm, late_hbm,
+    seg, keep, g1, bias1, ob, g2, bias2, c2, qb, vb, b1,
+    x, xn, wqkv, proj, att, scale_two, lse, delta, stat, mask, dy, ow, w1, w2, hidden, xhat, rstd, n2, n2t, z, da, act, di,
+    f1, f2, r1, r2, pa, pb, pc, pd, d_att, qg, biases, vec, late, early_buf, late_buf, *rest,
+):
+    rows, width = x.shape
+    half = rows // 2
+    heads = width // HEAD_DIM
+    cols = width
+    chunks = w2.shape[0] // cols
+    stage_bufs = list(rest[:-7])
+    sems, send_sems, recv_sems, core_send, core_recv, next_send, next_recv = rest[-7:]
+    at = place()
+    t = at["x"]
+    far, near = t * half, (1 - t) * half
+    own_rows, halo_rows, near_rows = pl.ds(0, rows), pl.ds(rows, half), pl.ds(half, half)
+    barrier = pltpu.get_barrier_semaphore()
+    for bit in BITS:
+        pl.semaphore_signal(barrier, inc=1, device_id=peer(at, bit), device_id_type=MESH)
+
+    def fetch(src, dst, i):
+        c = pltpu.make_async_copy(src, dst, sems.at[i])
+        c.start()
+        return c
+
+    small = ((seg_hbm, seg), (keep_hbm, keep), (g1_hbm, g1), (bias1_hbm, bias1), (ob_hbm, ob), (g2_hbm, g2), (bias2_hbm, bias2), (c2_hbm, c2), (qb_hbm, qb), (vb_hbm, vb), (b1_hbm, b1))
+    got_small = [fetch(src, dst, 6 + 2 * chunks + i) for i, (src, dst) in enumerate(small)]
+    got_x = [fetch(tok.at[pl.ds(far, half)], x.at[pl.ds(0, half)], 0), fetch(tok.at[pl.ds(near, half)], x.at[near_rows], 1)]
+    got_wqkv = fetch(wqkv_hbm, wqkv, 2)
+    got_dy = [fetch(dy_hbm.at[pl.ds(far, half)], dy.at[pl.ds(0, half)], 3), fetch(dy_hbm.at[pl.ds(near, half)], dy.at[near_rows], 4)]
+    got_ow = fetch(ow_hbm, ow, 5)
+    pl.semaphore_wait(barrier, len(BITS))
+    used = [0]
+
+    def job(bit, src, dst):
+        i, used[0] = used[0], used[0] + 1
+        return send(at, bit, src, dst, send_sems.at[i], recv_sems.at[i])
+
+    token_halo = job("x", tok.at[pl.ds(near, half)], xn.at[halo_rows])
+
+    for g in got_small:
+        g.wait()
+    starts = (t * (rows + half), t * rows + (1 - t) * half, (1 - t) * rows + t * half)
+    slots = [pl.ds(pl.multiple_of(s, 128), half) for s in starts]
+    ids = jnp.concatenate([seg[:, s] for s in slots], axis=1)
+    kept_row = jnp.concatenate([keep[:, s] for s in slots], axis=1)
+    key_row = jnp.where(kept_row == 1, ids, -1)
+    table = jnp.concatenate([ids, key_row, kept_row, jnp.zeros((5, rows + half), jnp.int32)], axis=0)
+    columns = jnp.transpose(table.astype(F32))
+    id_col, key_col, kept_col = columns[:, 0:1], columns[:, 1:2], columns[:, 2:3]
+    id_row, key_row = ids.astype(F32), key_row.astype(F32)
+    query_at = lax.broadcasted_iota(jnp.int32, (half, rows + half), 0)
+    key_at = lax.broadcasted_iota(jnp.int32, (half, rows + half), 1)
+    for part in range(2):
+        same = id_col[part * half : (part + 1) * half] == key_row
+        mask[pl.ds(part * half, half), :] = jnp.where(same | (query_at + part * half == key_at), 0.0, MASKED)
+    rstd[...] = jnp.broadcast_to(kept_col[:rows], rstd.shape)
+    for i in range(chunks):
+        biases[i : i + 1, :] = b1[i * cols : (i + 1) * cols].reshape(1, cols)
+    for i, ref in enumerate((g1, bias1, ob, g2, bias2, c2, qb, vb)):
+        biases[8 + i : 9 + i, :] = ref[...].reshape(1, width)
+    gain_one, bias_one, out_bias, gain_two, bias_two, fc2_bias = (biases[8 + i : 9 + i, :] for i in range(6))
+    vec[...] = jnp.zeros_like(vec)
+    late[...] = jnp.zeros_like(late)
+    vec[12:13, 0:128] = jnp.sum(rstd[...], axis=0, keepdims=True)
+    rb = 128
+
+    def normalize(src, dst, start, count):
+        def one(i, _):
+            rs = pl.ds(pl.multiple_of(start + i * rb, rb), rb)
+            v = src[rs, :].astype(F32)
+            centred = v - jnp.mean(v, axis=-1, keepdims=True)
+            var = jnp.mean(centred * centred, axis=-1, keepdims=True)
+            dst[rs, :] = (centred * lax.rsqrt(var + 1e-06) * gain_one + bias_one).astype(BF)
+            return 0
+
+        lax.fori_loop(0, count // rb, one, 0)
+
+    def project(start, count, which):
+        rs = pl.ds(start, count)
+        for j in which:
+            js = pl.ds(j * width, width)
+            v = mm(xn[rs, :], wqkv[:, js])
+            if j == 0:
+                proj[rs, js] = (v + biases[14:15, :]).astype(BF) * BF(HEAD_DIM ** (-0.5))
+            elif j == 1:
+                proj[rs, js] = v.astype(BF)
+            else:
+                proj[rs, js] = (v + biases[15:16, :]).astype(BF)
+
+    lane = lax.broadcasted_iota(jnp.int32, (1, PAIR), 1)
+
+    def cut(v, head):
+        return jnp.where((lane < HEAD_DIM) == (head == 0), v, 0).astype(BF)
+
+    def both(a, b):
+        return jnp.where(lane < HEAD_DIM, a, b)
+
+    def scores(p, query_rows, mask_rows, key_start, keys):
+        c = pl.multiple_of(p * PAIR, PAIR)
+        ks = pl.ds(key_start, keys)
+        q, k, v = proj[query_rows, pl.ds(c, PAIR)], proj[ks, pl.ds(width + c, PAIR)], proj[ks, pl.ds(2 * width + c, PAIR)]
+        total, new_tops = None, []
+        for head in range(2):
+            s = mm_nt(cut(q, head), k) + mask[mask_rows, ks]
+            top = jnp.max(s, axis=-1, keepdims=True)
+            e = jnp.exp(s - top).astype(BF)
+            ones = jnp.broadcast_to(cut(jnp.ones((1, PAIR), BF), head), (keys, PAIR))
+            part = mm(e, jnp.concatenate([cut(v, head), ones], axis=1))
+            total = part if total is None else total + part
+            new_tops.append(top)
+        return total[:, :PAIR], total[:, PAIR:], both(new_tops[0], new_tops[1])
+
+    def attended(p, rs, value, sums, tops):
+        c = pl.ds(pl.multiple_of(p * PAIR, PAIR), PAIR)
+        att[rs, c] = (value / sums).astype(BF)
+        hidden[rs, c] = tops + jnp.log(sums)
+
+    def attend_far(p, _):
+        rs = pl.ds(0, half)
+        attended(p, rs, *scores(p, rs, rs, 0, rows))
+        return 0
+
+    def attend_near(p, _):
+        c = pl.ds(pl.multiple_of(p * PAIR, PAIR), PAIR)
+        z[pl.ds(0, half), c], z[near_rows, c], da[near_rows, c] = scores(p, near_rows, near_rows, 0, rows)
+        return 0
+
+    def attend_halo(p, _):
+        c = pl.ds(pl.multiple_of(p * PAIR, PAIR), PAIR)
+        before = da[near_rows, c]
+        value, sums, after = scores(p, near_rows, near_rows, rows, half)
+        tops = jnp.maximum(before, after)
+        old, new = jnp.exp(before - tops), jnp.exp(after - tops)
+        attended(p, near_rows, value * new + z[pl.ds(0, half), c] * old, sums * new + z[near_rows, c] * old, tops)
+        return 0
+
+    for g in got_x:
+        g.wait()
+    normalize(x, xn, 0, rows)
+    got_wqkv.wait()
+    got_w = []
+    for c in range(chunks):
+        got_w.append(fetch(w1_hbm.at[:, pl.ds(c * cols, cols)], w1.at[:, pl.ds(c * cols, cols)], 6 + 2 * c))
+        got_w.append(fetch(w2_hbm.at[pl.ds(c * cols, cols)], w2.at[pl.ds(c * cols, cols)], 7 + 2 * c))
+    project(0, rows, (0, 1, 2))
+    lax.fori_loop(0, heads // 2, attend_far, 0, unroll=3)
+    lax.fori_loop(0, heads // 2, attend_near, 0, unroll=3)
+    token_halo.wait()
+    normalize(xn, xn, rows, half)
+    project(rows, half, (1, 2, 0))
+    lax.fori_loop(0, heads // 2, attend_halo, 0, unroll=3)
+    head_row = lax.broadcasted_iota(jnp.int32, (16, width), 0) * HEAD_DIM
+    lane_at = lax.broadcasted_iota(jnp.int32, (16, width), 1)
+    first = jnp.where(lane_at == head_row, 1.0, 0.0).astype(BF)
+    logs = hidden[...]
+    high = logs.astype(BF)
+    mid = (logs - high.astype(F32)).astype(BF)
+    low = (logs - high.astype(F32) - mid.astype(F32)).astype(BF)
+    lse[...] = mm_nt(first, high) + mm_nt(first, mid) + mm_nt(first, low)
+    got_ow.wait()
+
+    def add_vec(ref, i, v):
+        ref[i : i + 1, :] += jnp.sum(v, axis=0, keepdims=True)
+
+    def front(i, _):
+        rs = pl.ds(pl.multiple_of(i * rb, rb), rb)
+        branch = mm(att[rs, :], ow[...]) + out_bias
+        xs = x[rs, :].astype(F32)
+        h = xs + branch
+        hidden[rs, :] = h
+        kept = rstd[rs, :][:, 0:1]
+        add_vec(vec, 0, kept * xs * xs)
+        add_vec(vec, 1, kept * branch * branch)
+        centred = h - jnp.mean(h, axis=-1, keepdims=True)
+        r = lax.rsqrt(jnp.mean(centred * centred, axis=-1, keepdims=True) + 1e-06)
+        xh = centred * r
+        xhat[rs, :] = xh
+        scale_two[rs, :] = jnp.broadcast_to(r, (rb, PAIR))
+        n2[rs, :] = (xh * gain_two + bias_two).astype(BF)
+        return 0
+
+    lax.fori_loop(0, rows // rb, front, 0)
+    n2t[...] = jnp.transpose(n2[...])
+    for g in got_dy:
+        g.wait()
+
+    def core_copies(c):
+        hi, lo = c // 2, c % 2
+        other = 1 - at["core"]
+        pairs = ((f1.at[:, :, :, other], r1.at[hi, lo]), (f2.at[:, :, other], r2.at[hi, lo]))
+        return [
+            pltpu.make_async_remote_copy(s, d, core_send.at[i, c], core_recv.at[i, c], device_id=peer(at, "core"), device_id_type=MESH)
+            for i, (s, d) in enumerate(pairs)
+        ]
+
+    def next_copies(c):
+        hi, lo = c // 2, c % 2
+        jobs = (
+            ("x", r2.at[hi, lo, 1 - t, :, :, pl.ds(0, 256)], pa.at[hi, lo]),
+            ("y", r2.at[hi, lo, :, 1 - at["y"], :, pl.ds(256, 128)], pb.at[hi, lo]),
+            ("y", r1.at[hi, lo, :, :, 1 - at["y"], :, pl.ds(0, 256)], pc.at[hi, lo]),
+            ("z0", r1.at[hi, lo, :, 1 - at["z0"], :, :, pl.ds(256, 512)], pd.at[hi, lo]),
+        )
+        return [
+            pltpu.make_async_remote_copy(s, d, next_send.at[i, c], next_recv.at[i, c], device_id=peer(at, bit), device_id_type=MESH)
+            for i, (bit, s, d) in enumerate(jobs)
+        ]
+
+    def pass_on(c):
+        hi, lo = c // 2, c % 2
+        mine = at["core"]
+        for copy in core_copies(c):
+            copy.wait()
+
+        def one(i, _):
+            a, b, d = i // 4, i // 2 % 2, i % 2
+            r1[hi, lo, a, b, d] += f1[a, b, d, mine]
+            return 0
+
+        lax.fori_loop(0, 8, one, 0, unroll=2)
+
+        def two(i, _):
+            r2[hi, lo, i // 2, i % 2] += f2[i // 2, i % 2, mine]
+            return 0
+
+        lax.fori_loop(0, 4, two, 0)
+        for copy in next_copies(c):
+            copy.start()
+
+    def chunk(c, _):
+        for i in range(2):
+            pltpu.make_async_copy(w2_hbm.at[pl.ds(0, cols)], w2.at[pl.ds(0, cols)], sems.at[6 + 2 * c + i]).wait()
+        here = pl.ds(pl.multiple_of(c * cols, cols), cols)
+        z[...] = mm(n2[...], w1[:, here]) + biases[pl.ds(c, 1), :]
+        da[...] = mm_nt(dy[...], w2[here, :])
+        gr = 64
+        bsum = jnp.zeros((1, cols), F32)
+        for i in range(rows // gr):
+            rs = pl.ds(i * gr, gr)
+            a, s = gelu_and_slope(z[rs, :])
+            act[rs, here] = a.astype(BF)
+            d = (da[rs, :] * s).astype(BF)
+            di[rs, here] = d
+            bsum = bsum + jnp.sum(d.astype(F32), axis=0, keepdims=True)
+        vec[pl.ds(8 + c, 1), :] = bsum
+
+        @pl.when(c > 0)
+        def _():
+            pass_on(c - 1)
+
+        f1[...] = mm(n2t[...], di[:, here]).astype(BF).reshape(f1.shape)
+        g = mm_tn(act[:, here], dy[...]).astype(BF)
+        f2[0] = g[:, : width // 2].reshape(f2.shape[1:])
+        f2[1] = g[:, width // 2 :].reshape(f2.shape[1:])
+        for copy in core_copies(c):
+            copy.start()
+        return 0
+
+    lax.fori_loop(0, chunks, chunk, 0)
+    da[...] = mm_nt(di[...], w1[...])
+    pass_on(chunks - 1)
+
+    def middle(i, _):
+        rs = pl.ds(pl.multiple_of(i * rb, rb), rb)
+        g = da[rs, :]
+        xh = xhat[rs, :]
+        add_vec(vec, 4, g * xh)
+        add_vec(vec, 5, g)
+        gy = g * gain_two
+        mean_gy = jnp.mean(gy, axis=-1, keepdims=True)
+        mean_gx = jnp.mean(gy * xh, axis=-1, keepdims=True)
+        dys = dy[rs, :].astype(F32)
+        add_vec(vec, 7, dys)
+        dh = dys + scale_two[rs, :][:, 0:1] * (gy - mean_gy - xh * mean_gx)
+        xhat[rs, :] = dh
+        low = dh.astype(BF)
+        n2[rs, :] = low
+        add_vec(vec, 6, low.astype(F32))
+        return 0
+
+    lax.fori_loop(0, rows // rb, middle, 0)
+    d_att[own_rows, :] = mm_nt(n2[...], ow[...]).astype(BF)
+    mine = jnp.where((lane_at >= head_row) & (lane_at < head_row + HEAD_DIM), 1.0, 0.0).astype(BF)
+    prod = d_att[own_rows, :].astype(F32) * att[...].astype(F32)
+    hi = prod.astype(BF)
+    lo = (prod - hi.astype(F32)).astype(BF)
+    delta[...] = mm_nt(mine, hi) + mm_nt(mine, lo)
+    halos = [
+        job("x", d_att.at[near_rows], d_att.at[halo_rows]),
+        job("x", lse.at[:, near_rows], stat.at[0]),
+        job("x", delta.at[:, near_rows], stat.at[1]),
+    ]
+
+    def share(ref, dims, order):
+        bufs = [stage_bufs.pop(0) for _ in order]
+        first, used[0] = used[0], used[0] + len(order)
+        return Share(at, ref, dims, order, bufs, send_sems, recv_sems, first)
+
+    og = qg.at[2]
+    A, B, C, D = (share(ref, *part) for ref, part in ((pa, PART_A), (pb, PART_B), (pc, PART_C), (pd, PART_D)))
+    O = share(og, MATRIX, OUT_ORDER)
+    Q = [share(qg.at[i], MATRIX, ORDERS[i]) for i in range(3)]
+    early = Total(at, vec, early_buf, send_sems, recv_sems, used[0])
+    later = Total(at, late, late_buf, send_sems, recv_sems, used[0] + 5)
+    early.start()
+    def settle(c, _):
+        hi, lo = c // 2, c % 2
+        for copy in next_copies(c):
+            copy.wait()
+        for i in range(2):
+            pa[hi, lo, i] += r2[hi, lo, t, i, :, 0:256]
+            pb[hi, lo, i] += r2[hi, lo, i, at["y"], :, 256:384]
+            for j in range(2):
+                pc[hi, lo, i, j] += r1[hi, lo, i, j, at["y"], :, 0:256]
+                pd[hi, lo, i, j] += r1[hi, lo, i, at["z0"], j, :, 256:768]
+        return 0
+
+    n2t[...] = jnp.transpose(att[...])
+    for i in range(2):
+        og_half = mm(n2t[...], n2[:, i * (width // 2) : (i + 1) * (width // 2)]).astype(BF)
+        og[:, :, :, :, i] = og_half.reshape((2, 2, 2, 2) + og.shape[-2:])
+    O.start()
+
+    key_at = lax.broadcasted_iota(jnp.int32, (half, rows), 0)
+    query_at = lax.broadcasted_iota(jnp.int32, (half, rows), 1)
+    for part in range(2):
+        same = key_col[part * half : (part + 1) * half] == id_row[:, :rows]
+        mask[pl.ds(part * half, half), pl.ds(0, rows)] = jnp.where(same | (query_at == key_at + part * half), 0.0, MASKED)
+    mask[pl.ds(0, half), halo_rows] = jnp.where(key_col[half:rows] == id_row[:, rows:], 0.0, MASKED)
+    mask[near_rows, halo_rows] = jnp.where(key_col[rows:] == id_row[:, half:rows], 0.0, MASKED)
+
+    def own(p, _):
+        c = pl.multiple_of(p * PAIR, PAIR)
+        col, kcol, vcol = pl.ds(c, PAIR), pl.ds(width + c, PAIR), pl.ds(2 * width + c, PAIR)
+        q, k, v = proj[own_rows, col], proj[:, kcol], proj[:, vcol]
+        do = d_att[own_rows, col]
+        gq = gk = gv = gn = None
+        for head in range(2):
+            qh, kh, doh = cut(q, head), cut(k, head), cut(do, head)
+            ls = lse[pl.ds(2 * p + head, 1), :]
+            de = delta[pl.ds(2 * p + head, 1), :]
+            prob = jnp.exp(mm_nt(k[:rows], qh) + mask[:, pl.ds(0, rows)] - ls)
+            ds = (prob * (mm_nt(v[:rows], doh) - de)).astype(BF)
+            a = mm(prob.astype(BF), doh)
+            b = mm(ds, qh)
+            c = mm_tn(ds, kh[:rows])
+            prob = jnp.exp(mm_nt(k[rows:], qh[half:]) + mask[near_rows, halo_rows] - ls[:, half:])
+            ds = (prob * (mm_nt(v[rows:], doh[half:]) - de[:, half:])).astype(BF)
+            d = mm_tn(ds, kh[rows:])
+            gv = a if gv is None else gv + a
+            gk = b if gk is None else gk + b
+            gq = c if gq is None else gq + c
+            gn = d if gn is None else gn + d
+        scale = HEAD_DIM ** (-0.5)
+        di[pl.ds(0, half), col] = (gq[:half] * scale).astype(BF)
+        di[near_rows, col] = ((gq[half:] + gn) * scale).astype(BF)
+        di[pl.ds(0, half), kcol] = gk[:half].astype(BF)
+        di[pl.ds(0, half), vcol] = gv[:half].astype(BF)
+        z[pl.ds(0, half), col] = gk[half:]
+        z[near_rows, col] = gv[half:]
+        return 0
+
+    def halo(p, _):
+        c = pl.multiple_of(p * PAIR, PAIR)
+        col, kcol, vcol = pl.ds(c, PAIR), pl.ds(width + c, PAIR), pl.ds(2 * width + c, PAIR)
+        q, k, v = proj[halo_rows, col], proj[near_rows, kcol], proj[near_rows, vcol]
+        do = d_att[halo_rows, col]
+        gk, gv = z[pl.ds(0, half), col], z[near_rows, col]
+        for head in range(2):
+            qh, doh = cut(q, head), cut(do, head)
+            ls = stat[0, pl.ds(2 * p + head, 1), :]
+            de = stat[1, pl.ds(2 * p + head, 1), :]
+            prob = jnp.exp(mm_nt(k, qh) + mask[pl.ds(0, half), halo_rows] - ls)
+            ds = (prob * (mm_nt(v, doh) - de)).astype(BF)
+            gv = gv + mm(prob.astype(BF), doh)
+            gk = gk + mm(ds, qh)
+        di[near_rows, kcol] = gk.astype(BF)
+        di[near_rows, vcol] = gv.astype(BF)
+        return 0
+
+    n2t[...] = jnp.transpose(xn[own_rows, :])
+    early.step()
+    lax.fori_loop(0, 2, own, 0, unroll=2)
+    lax.fori_loop(0, chunks, settle, 0)
+    for s in (A, B, C, D):
+        s.start()
+    O.step()
+    early.step()
+    lax.fori_loop(2, heads // 2, own, 0, unroll=2)
+    for h in halos:
+        h.wait()
+    lax.fori_loop(0, heads // 2, halo, 0, unroll=3)
+    early.step()
+    third = width // 2
+
+    def weigh(j):
+        g = mm(n2t[...], di[:, pl.ds(j * width, width)]).astype(BF)
+        for i in range(2):
+            side, part = divmod(2 * j + i, 3)
+            qg[part, :, :, :, :, side] = g[:, i * third : (i + 1) * third].reshape((2, 2, 2, 2) + qg.shape[-2:])
+
+    weigh(0)
+    weigh(1)
+    Q[0].start()
+    weigh(2)
+    Q[1].start()
+    Q[2].start()
+    early.step()
+    da[...] = mm_nt(di[:, pl.ds(0, 3 * width)], wqkv[...])
+    for s in (A, B, C, D):
+        s.step()
+    for s in Q:
+        s.step()
+    O.step()
+    z[...] = mm(act[...], w2[...])
+
+    def back(i, _):
+        rs = pl.ds(pl.multiple_of(i * rb, rb), rb)
+        xs = x[rs, :].astype(F32)
+        centred = xs - jnp.mean(xs, axis=-1, keepdims=True)
+        r = lax.rsqrt(jnp.mean(centred * centred, axis=-1, keepdims=True) + 1e-06)
+        xh = centred * r
+        g = da[rs, :]
+        add_vec(late, 0, g * xh)
+        add_vec(late, 1, g)
+        gy = g * gain_one
+        mean_gy = jnp.mean(gy, axis=-1, keepdims=True)
+        mean_gx = jnp.mean(gy * xh, axis=-1, keepdims=True)
+        w1[rs, pl.ds(width, width)] = (xhat[rs, :] + r * (gy - mean_gy - xh * mean_gx)).astype(BF)
+        add_vec(late, 2, di[rs, pl.ds(0, width)].astype(F32))
+        add_vec(late, 3, di[rs, pl.ds(2 * width, width)].astype(F32))
+        branch = z[rs, :] + fc2_bias
+        result = hidden[rs, :] + branch
+        w1[rs, pl.ds(0, width)] = result.astype(BF)
+        kept = rstd[rs, :][:, 0:1]
+        add_vec(late, 4, kept * branch * branch)
+        add_vec(late, 5, kept * result * result)
+        return 0
+
+    lax.fori_loop(0, rows // rb, back, 0)
+    later.start()
+    copies = [
+        fetch(w1.at[pl.ds(0, half), pl.ds(0, width)], out_hbm.at[pl.ds(far, half)], 0),
+        fetch(w1.at[near_rows, pl.ds(0, width)], out_hbm.at[pl.ds(near, half)], 1),
+        fetch(w1.at[pl.ds(0, half), pl.ds(width, width)], gt_hbm.at[pl.ds(far, half)], 2),
+        fetch(w1.at[near_rows, pl.ds(width, width)], gt_hbm.at[pl.ds(near, half)], 3),
+    ]
+
+    block, wide = width // 16, w2.shape[0] // 16
+
+    def put_a(_, v):
+        z[pl.ds(0, wide), 0:256] = v
+
+    def put_b(_, v):
+        z[pl.ds(0, wide), 256:384] = v
+
+    def put_c(i, v):
+        z[pl.ds(wide + i[0] * block, block), 0:256] = v
+
+    def put_d(i, v):
+        z[pl.ds(wide + i[0] * block, block), 256:768] = v
+
+    def put_o(_, v):
+        z[pl.ds(wide + 2 * block, block), 0:384] = v
+
+    early.finish()
+    copies.append(fetch(early.ref, vec_hbm, 4))
+    for s in (A, B, C, D):
+        s.step()
+    O.step()
+    for s in Q:
+        s.step()
+    later.step()
+    for s in Q:
+        s.step()
+    later.step()
+    O.step()
+    for s in Q:
+        s.step()
+    later.step()
+    for s, put in ((A, put_a), (B, put_b), (C, put_c), (D, put_d)):
+        s.last(put)
+    O.last(put_o)
+    copies += [
+        fetch(z.at[pl.ds(0, wide), pl.ds(0, width // 2)], fc2_hbm, 5),
+        fetch(z.at[pl.ds(wide, block)], fc1_hbm.at[:, pl.ds(0, width)], 6),
+        fetch(z.at[pl.ds(wide + block, block)], fc1_hbm.at[:, pl.ds(width, width)], 7),
+        fetch(z.at[pl.ds(wide + 2 * block, block), pl.ds(0, width // 2)], o_hbm, 8),
+    ]
+    later.step()
+    for i in range(3):
+
+        def put_q(_, v, i=i):
+            da[pl.ds(i * block, block), 0:384] = v
+
+        Q[i].last(put_q)
+        copies.append(fetch(da.at[pl.ds(i * block, block), pl.ds(0, third)], qkv_hbm.at[:, pl.ds(i * third, third)], 10 + i))
+    later.finish()
+    copies.append(fetch(later.ref, late_hbm, 9))
+    for c in copies:
+        c.wait()
+
+
+def call_everything(tokens, seg, keep, g1, bias1, wqkv, qb, vb, ow, ob, g2, bias2, w1, b1, w2, c2, dy):
+    rows, width = tokens.shape
+    half = rows // 2
+    hid = w1.shape[1]
+    chunks = hid // width
+    block, wide = width // 16, hid // 16
+    sds = jax.ShapeDtypeStruct
+    V = pltpu.VMEM
+    parts = ((2, 2, 2, wide, 256), (2, 2, 2, wide, 128), (2, 2, 2, 2, block, 256), (2, 2, 2, 2, block, 512))
+    stages = (
+        stage_shapes(*PART_A, wide, 256)
+        + stage_shapes(*PART_B, wide, 128)
+        + stage_shapes(*PART_C, block, 256)
+        + stage_shapes(*PART_D, block, 512)
+        + stage_shapes(MATRIX, OUT_ORDER, block, width // 2)
+        + [s for order in ORDERS for s in stage_shapes(MATRIX, order, block, width // 2)]
+    )
+    jobs = 4 + len(stages) + 10
+    DMA = pltpu.SemaphoreType.DMA
+    return pl.pallas_call(
+        everything,
+        out_shape=(
+            sds((rows, width), BF), sds((rows, width), BF), sds((block, 3 * width // 2), F32), sds((block, width // 2), F32),
+            sds((block, hid // 2), F32), sds((wide, width // 2), F32), sds((16, width), F32), sds((8, width), F32),
+        ),
+        in_specs=[any_spec()] * 17,
+        out_specs=(any_spec(),) * 8,
+        scratch_shapes=[V(seg.shape, jnp.int32), V(keep.shape, jnp.int32)] + [V((width,), F32)] * 8 + [
+            V((hid,), F32),
+            V((rows, width), BF), V((rows + half, width), BF), V((width, 3 * width), BF), V((rows + half, 3 * width), BF),
+            V((rows, width), BF), V((rows, PAIR), F32), V((16, rows), F32), V((16, rows), F32), V((2, 16, half), F32),
+            V((rows, rows + half), F32), V((rows, width), BF), V((width, width), BF), V((width, hid), BF), V((hid, width), BF),
+            V((rows, width), F32), V((rows, width), F32), V((rows, PAIR), F32), V((rows, width), BF), V((width, rows), BF),
+            V((rows, width), F32), V((rows, width), F32), V((rows, hid), BF), V((rows, hid), BF),
+            V((2, 2, 2, 2, block, width), BF), V((2, 2, 2, wide, width // 2), BF),
+            V((2, 2, 2, 2, 2, block, width), BF), V((2, 2, 2, 2, wide, width // 2), BF),
+        ] + [V(s, BF) for s in parts] + [
+            V((rows + half, width), BF), V((3, 2, 2, 2, 2, 2, block, width // 2), BF),
+            V((16, width), F32), V((16, width), F32), V((8, width), F32), V((5, 16, width), F32), V((5, 8, width), F32),
+        ] + [V(s, BF) for s in stages] + [
+            DMA((17 + 2 * chunks,)), DMA((jobs,)), DMA((jobs,)),
+            DMA((2, chunks)), DMA((2, chunks)), DMA((4, chunks)), DMA((4, chunks)),
+        ],
+        compiler_params=pltpu.CompilerParams(collective_id=0, has_side_effects=True, vmem_limit_bytes=67043328),
+        name="everything",
+    )(tokens, seg, keep, g1, bias1, wqkv, qb, vb, ow, ob, g2, bias2, w1, b1, w2, c2, dy)
+
+
+def finish(*refs):
+    ins, outs, bufs, sems = refs[:8], refs[8:24], refs[24:-1], refs[-1]
+    loads = [pltpu.make_async_copy(src, buf, sems.at[i]) for i, (src, buf) in enumerate(zip(ins, bufs[:8]))]
+    for c in loads:
+        c.start()
+    vec, late = bufs[6:8]
+    lines = bufs[8:]
+    width = lines[0].shape[0]
+    out, gt, g1, b1, qkv, qb, vb, o, ob, g2, b2, f1, f1b, f2, f2b, rm = outs
+    stores = []
+
+    def store(src, dst):
+        c = pltpu.make_async_copy(src, dst, sems.at[8 + len(stores)])
+        c.start()
+        stores.append(c)
+
+    loads[6].wait()
+    loads[7].wait()
+    rows = ((g1, late, 0), (b1, late, 1), (qb, late, 2), (vb, late, 3), (ob, vec, 6), (g2, vec, 4), (b2, vec, 5), (f2b, vec, 7))
+    for (dst, src, i), line in zip(rows, lines):
+        line[...] = src[i, :]
+        store(line, dst)
+    for i in range(4):
+        lines[8][pl.ds(i * width, width)] = vec[8 + i, :]
+    store(lines[8], f1b)
+    squares = jnp.concatenate([vec[0:2, :], late[4:6, :]], axis=0)
+    ratio = jnp.sqrt(jnp.sum(squares, axis=1, keepdims=True) / (vec[12:13, 0:1] * width))
+    diagonal = lax.broadcasted_iota(jnp.int32, (4, 128), 0) == lax.broadcasted_iota(jnp.int32, (4, 128), 1)
+    lines[9][...] = jnp.sum(jnp.where(diagonal, ratio, 0.0), axis=0, keepdims=True)
+    store(lines[9], rm)
+    for i, dst in enumerate((out, gt, qkv, o, f1, f2)):
+        loads[i].wait()
+        store(bufs[i], dst)
+    for c in stores:
+        c.wait()
+
+
+def call_finish(out, gt, qkv, o, f1, f2, vec, late, hid):
+    width = out.shape[1]
+    sds = jax.ShapeDtypeStruct
+    line = sds((width,), F32)
+    shapes = (
+        sds(out.shape, BF), sds(gt.shape, BF), line, line, sds(qkv.shape, F32), line, line, sds(o.shape, F32), line, line, line,
+        sds(f1.shape, F32), sds((hid,), F32), sds(f2.shape, F32), line, sds((1, 128), F32),
+    )
+    args = (out, gt, qkv, o, f1, f2, vec, late)
+    return pl.pallas_call(
+        finish,
+        out_shape=shapes,
+        in_specs=[any_spec()] * 8,
+        out_specs=(any_spec(),) * 16,
+        scratch_shapes=[pltpu.VMEM(v.shape, v.dtype) for v in args] + [pltpu.VMEM((width,), F32)] * 8
+        + [pltpu.VMEM((hid,), F32), pltpu.VMEM((1, 128), F32), pltpu.SemaphoreType.DMA((24,))],
+        name="finish",
+    )(*args)
 
 
 def layer_norm(values, norm_gain, norm_bias):
@@ -17,7 +757,7 @@
     return jax.nn.gelu(values, approximate=False)
 
 
-def on_device(
+def on_device_general(
     tokens,
     segment_ids,
     keep_mask,
@@ -266,47 +1006,28 @@
     )
 
 
+def on_device(tokens, segment_ids, keep_mask, gain_one, bias_one, qkv_weight, query_bias, value_bias, out_weight, out_bias, gain_two, bias_two, fc1_weight, fc1_bias, fc2_weight, fc2_bias, cotangent):
+    out, gt, qg, og, f1, f2, vec, late = call_everything(
+        tokens[0], segment_ids, keep_mask, gain_one, bias_one, qkv_weight, query_bias, value_bias, out_weight, out_bias,
+        gain_two, bias_two, fc1_weight, fc1_bias, fc2_weight, fc2_bias, cotangent[0],
+    )
+    r = list(call_finish(out, gt, qg, og, f1, f2, vec, late, fc1_weight.shape[1]))
+    r[0] = r[0][None]
+    r[1] = r[1][None]
+    r[15] = r[15][0, :4]
+    return tuple(r)
+
+
+def fits(mesh):
+    return mesh.shape["tile"] == 2 and mesh.shape["dp"] == 16
+
+
 def solution(mesh):
-    placed = (
-        P("dp", "tile", None),
-        P("dp", None),
-        P("dp", None),
-        P(),
-        P(),
-        P(),
-        P(),
-        P(),
-        P(),
-        P(),
-        P(),
-        P(),
-        P(),
-        P(),
-        P(),
-        P(),
-        P("dp", "tile", None),
-    )
+    S, D, T = P("dp", "tile", None), P("dp", None), P("dp", "tile")
     return jax.shard_map(
-        on_device,
+        on_device if fits(mesh) else on_device_general,
         mesh=mesh,
-        in_specs=placed,
-        out_specs=(
-            P("dp", "tile", None),
-            P("dp", "tile", None),
-            P(),
-            P(),
-            P("dp", "tile"),
-            P(),
-            P(),
-            P("dp", "tile"),
-            P(),
-            P(),
-            P(),
-            P("dp", "tile"),
-            P(),
-            P("dp", "tile"),
-            P(),
-            P(),
-        ),
+        in_specs=(S, D, D) + (P(),) * 13 + (S,),
+        out_specs=(S, S, P(), P(), T, P(), P(), T, P(), P(), P(), T, P(), T, P(), P()),
         check_vma=False,
     )

time: 609 us -> 118 us (0.19); the launches traced: 602 us -> 118 us
  waiting for transfers between devices: 301 us -> 0 us
  matrix products: 135 us -> 0 us
  Pallas kernels: 0 us -> 116 us
  local copies, waits for them, and re-layouts: 57.3 us -> 1.11 us
  other arithmetic: 50.4 us -> 0 us
  blocking collectives: 41.5 us -> 0 us
  between operations: 16 us -> 0.67 us
    reduce_scatter x6 -> x0, waiting for transfers between devices: 256 us -> none  [the longest x1 76.8 us: on_device(): lax.psum_scatter(matrices[3].astype(jnp.bfloat16), 'dp', scatter_dimensio...]
    dot_general x30 -> x0, matrix products: 135 us -> none  [the longest x3 21.2 us: on_device(): jnp.einsum('sqhe,skhe->shqk', grad_part, value_part, preferred_element_ty...]
    pallas_call x0 -> x2, Pallas kernels: none -> 116 us  [the longest x1 113 us: call_everything(): pl.pallas_call(everything, out_shape=(sds((rows, width), BF), sds((rows,...]
    psum x1 -> x0, blocking collectives: 41.5 us -> none  [on_device(): lax.psum((gain_one_grad, bias_one_grad, query_bias_grad, value_bias_grad,...]
    all_gather x1 -> x0, waiting for transfers between devices: 37.7 us -> none  [on_device(): shared_all = lax.all_gather(shared_local, 'tile', axis=1, tiled=True)]
    slice x18 -> x0, local copies, waits for them, and re-layouts: 32.1 us -> none  [the longest x15 29.6 us: split_heads(): sliced = source[..., column:column + head_block]]
    convert_element_type x7 -> x0, other arithmetic: 22.6 us -> none  [the longest x3 16.3 us: on_device(): grad_scores = (probs_again * (grad_probs - centre)).astype(jnp.bfloat16)]
    unnamed x158 -> x0, local copies, waits for them, and re-layouts: 21.5 us -> none
  transfers between devices with their start and end apart: 10 -> 0, of which waited for: 7 -> 0; matrix products, arithmetic and copies ran while one was open for 16% -> 0% of each run, Pallas kernels for 0% -> 0%
where the time goes in v2:
time: 118 us
  Pallas kernels  116 us (98%)
    pallas_call x1, Pallas kernels, call_everything(): pl.pallas_call(everything, out_shape=(sds((rows, width), BF), sds((rows,...  113 us
    pallas_call x1, Pallas kernels, call_finish(): pl.pallas_call(finish, out_shape=shapes, in_specs=[any_spec()] * 8, out_s...  3.37 us

profile of v2, /device:TPU:0, one launch (start us, length us, event | category | flops | bytes accessed | tf_op | source)
XLA Modules:
  0.0 118.0 jit_solution(10874995199608224666)
XLA Ops:
  0.7 112.9 %everything.1 = (bf16[512,768]{1,0:T(8,128)(2,1)}, bf16[512,768]{1,0:T(8,128)(2,1)}, f32[48,1152]{1,0:T(8,128)}, f32[48,384]{1,0:T(8,128)}, f32[48,1536]{1,0:T(8...) custom-call(bf16[512,768]{1,0:T(8,128)(2,1)} %bitcast.6, s32[1,1024]{1,0:T(1,128)} %seg_hbm.1, ...), custom_call_target="tpu_custom_call" | custom-call | tf_op jit(solution)/shard_map/everything/pallas_call | solution.py:663
  113.5 3.4 %finish.1 = (bf16[512,768]{1,0:T(8,128)(2,1)}, bf16[512,768]{1,0:T(8,128)(2,1)}, f32[768]{0:T(1024)}, f32[768]{0:T(1024)}, f32[48,1152]{1,0:T(8,128)}, /*index=5...) custom-call(bf16[512,768]{1,0:T(8,128)(2,1)} %get-tuple-element.40.r, ...), custom_call_target="tpu_custom_call" | custom-call | tf_op jit(solution)/shard_map/finish/pallas_call | solution.py:738
  116.9 1.1 slice_bitcast_fusion

commit v3 on v2

--- a/solution.py
+++ b/solution.py
@@ -117,14 +117,14 @@
         self.start()
 
 
-BITS = ("core", "y", "z0", "z1", "x")
+BITS = ("core", "z1", "y", "z0", "x")
 PART_A = (("z1", "z0", "y"), ("z0", "y", "z1"))
 PART_B = (("z1", "z0", "x"), ("x", "z0", "z1"))
 PART_C = (("x", "j", "z1", "z0"), ("z0", "x", "z1"))
 PART_D = (("x", "j", "z1", "y"), ("y", "x", "z1"))
 MATRIX = ("z1", "z0", "y", "core", "x")
 ORDERS = (("core", "x", "y", "z0", "z1"), ("core", "y", "z0", "x", "z1"), ("core", "z0", "x", "y", "z1"))
-OUT_ORDER = ("core", "y", "z0", "x", "z1")
+OUT_ORDER = ("core", "x", "y", "z0", "z1")
 
 
 def stage_shapes(dims, order, rows, cols):
@@ -166,8 +166,6 @@
     got_small = [fetch(src, dst, 6 + 2 * chunks + i) for i, (src, dst) in enumerate(small)]
     got_x = [fetch(tok.at[pl.ds(far, half)], x.at[pl.ds(0, half)], 0), fetch(tok.at[pl.ds(near, half)], x.at[near_rows], 1)]
     got_wqkv = fetch(wqkv_hbm, wqkv, 2)
-    got_dy = [fetch(dy_hbm.at[pl.ds(far, half)], dy.at[pl.ds(0, half)], 3), fetch(dy_hbm.at[pl.ds(near, half)], dy.at[near_rows], 4)]
-    got_ow = fetch(ow_hbm, ow, 5)
     pl.semaphore_wait(barrier, len(BITS))
     used = [0]
 
@@ -213,7 +211,7 @@
             dst[rs, :] = (centred * lax.rsqrt(var + 1e-06) * gain_one + bias_one).astype(BF)
             return 0
 
-        lax.fori_loop(0, count // rb, one, 0)
+        lax.fori_loop(0, count // rb, one, 0, unroll=2)
 
     def project(start, count, which):
         rs = pl.ds(start, count)
@@ -278,6 +276,8 @@
         g.wait()
     normalize(x, xn, 0, rows)
     got_wqkv.wait()
+    got_dy = [fetch(dy_hbm.at[pl.ds(far, half)], dy.at[pl.ds(0, half)], 3), fetch(dy_hbm.at[pl.ds(near, half)], dy.at[near_rows], 4)]
+    got_ow = fetch(ow_hbm, ow, 5)
     got_w = []
     for c in range(chunks):
         got_w.append(fetch(w1_hbm.at[:, pl.ds(c * cols, cols)], w1.at[:, pl.ds(c * cols, cols)], 6 + 2 * c))
@@ -287,7 +287,7 @@
     lax.fori_loop(0, heads // 2, attend_near, 0, unroll=3)
     token_halo.wait()
     normalize(xn, xn, rows, half)
-    project(rows, half, (1, 2, 0))
+    project(rows, half, (1, 2))
     lax.fori_loop(0, heads // 2, attend_halo, 0, unroll=3)
     head_row = lax.broadcasted_iota(jnp.int32, (16, width), 0) * HEAD_DIM
     lane_at = lax.broadcasted_iota(jnp.int32, (16, width), 1)
@@ -319,7 +319,7 @@
         n2[rs, :] = (xh * gain_two + bias_two).astype(BF)
         return 0
 
-    lax.fori_loop(0, rows // rb, front, 0)
+    lax.fori_loop(0, rows // rb, front, 0, unroll=2)
     n2t[...] = jnp.transpose(n2[...])
     for g in got_dy:
         g.wait()
@@ -519,18 +519,18 @@
         return 0
 
     n2t[...] = jnp.transpose(xn[own_rows, :])
+    project(rows, half, (0,))
+    lax.fori_loop(0, 2, own, 0, unroll=2)
     early.step()
-    lax.fori_loop(0, 2, own, 0, unroll=2)
+    O.step()
     lax.fori_loop(0, chunks, settle, 0)
-    for s in (A, B, C, D):
+    for s in (B, C, A, D):
         s.start()
-    O.step()
+    lax.fori_loop(2, heads // 2, own, 0, unroll=2)
     early.step()
-    lax.fori_loop(2, heads // 2, own, 0, unroll=2)
     for h in halos:
         h.wait()
     lax.fori_loop(0, heads // 2, halo, 0, unroll=3)
-    early.step()
     third = width // 2
 
     def weigh(j):
@@ -545,14 +545,14 @@
     weigh(2)
     Q[1].start()
     Q[2].start()
+    z[...] = mm(act[...], w2[...])
     early.step()
-    da[...] = mm_nt(di[:, pl.ds(0, 3 * width)], wqkv[...])
-    for s in (A, B, C, D):
+    for s in (B, C, A, D):
         s.step()
     for s in Q:
         s.step()
     O.step()
-    z[...] = mm(act[...], w2[...])
+    da[...] = mm_nt(di[:, pl.ds(0, 3 * width)], wqkv[...])
 
     def back(i, _):
         rs = pl.ds(pl.multiple_of(i * rb, rb), rb)
@@ -603,21 +603,20 @@
     def put_o(_, v):
         z[pl.ds(wide + 2 * block, block), 0:384] = v
 
+    early.step()
+    later.step()
+    for s in (B, C, A, D):
+        s.step()
+    for _ in range(3):
+        for s in Q:
+            s.finish()
+        later.step()
+        for s in Q:
+            s.start()
+        if O.order:
+            O.step()
     early.finish()
     copies.append(fetch(early.ref, vec_hbm, 4))
-    for s in (A, B, C, D):
-        s.step()
-    O.step()
-    for s in Q:
-        s.step()
-    later.step()
-    for s in Q:
-        s.step()
-    later.step()
-    O.step()
-    for s in Q:
-        s.step()
-    later.step()
     for s, put in ((A, put_a), (B, put_b), (C, put_c), (D, put_d)):
         s.last(put)
     O.last(put_o)
@@ -627,7 +626,6 @@
         fetch(z.at[pl.ds(wide + block, block)], fc1_hbm.at[:, pl.ds(width, width)], 7),
         fetch(z.at[pl.ds(wide + 2 * block, block), pl.ds(0, width // 2)], o_hbm, 8),
     ]
-    later.step()
     for i in range(3):
 
         def put_q(_, v, i=i):

time: 118 us -> 108 us (0.915); the launches traced: 118 us -> 106 us
  Pallas kernels: 116 us -> 105 us
    pallas_call x1, Pallas kernels: 113 us -> 101 us  [call_everything(): pl.pallas_call(everything, out_shape=(sds((rows, width), BF), sds((rows,...]
where the time goes in v3:
time: 108 us; the launch traced here: 106 us
  Pallas kernels  105 us (97%)
  local copies, waits for them, and re-layouts  1.11 us (1%)
    pallas_call x1, Pallas kernels, call_everything(): pl.pallas_call(everything, out_shape=(sds((rows, width), BF), sds((rows,...  101 us
    pallas_call x1, Pallas kernels, call_finish(): pl.pallas_call(finish, out_shape=shapes, in_specs=[any_spec()] * 8, out_s...  3.37 us

profile of v3, /device:TPU:0, one launch (start us, length us, event | category | flops | bytes accessed | tf_op | source)
XLA Modules:
  0.0 106.3 jit_solution(16003334677581909584)
XLA Ops:
  0.7 101.2 %everything.1 = (bf16[512,768]{1,0:T(8,128)(2,1)}, bf16[512,768]{1,0:T(8,128)(2,1)}, f32[48,1152]{1,0:T(8,128)}, f32[48,384]{1,0:T(8,128)}, f32[48,1536]{1,0:T(8...) custom-call(bf16[512,768]{1,0:T(8,128)(2,1)} %bitcast.6, s32[1,1024]{1,0:T(1,128)} %seg_hbm.1, ...), custom_call_target="tpu_custom_call" | custom-call | tf_op jit(solution)/shard_map/everything/pallas_call | solution.py:661
  101.8 3.4 %finish.1 = (bf16[512,768]{1,0:T(8,128)(2,1)}, bf16[512,768]{1,0:T(8,128)(2,1)}, f32[768]{0:T(1024)}, f32[768]{0:T(1024)}, f32[48,1152]{1,0:T(8,128)}, /*index=5...) custom-call(bf16[512,768]{1,0:T(8,128)(2,1)} %get-tuple-element.40.r, ...), custom_call_target="tpu_custom_call" | custom-call | tf_op jit(solution)/shard_map/finish/pallas_call | solution.py:736
  105.2 1.1 %slice_bitcast_fusion = f32[4]{0:T(128)} fusion(f32[1,128]{1,0:T(1,128)} %get-tuple-element.63), kind=kLoop, calls=%fused_computation | loop fusion | bytes 32 | tf_op jit(solution)/shard_map/squeeze | solution.py:1015

commit v4 on v3

--- a/solution.py
+++ b/solution.py
@@ -714,9 +714,8 @@
     store(lines[8], f1b)
     squares = jnp.concatenate([vec[0:2, :], late[4:6, :]], axis=0)
     ratio = jnp.sqrt(jnp.sum(squares, axis=1, keepdims=True) / (vec[12:13, 0:1] * width))
-    diagonal = lax.broadcasted_iota(jnp.int32, (4, 128), 0) == lax.broadcasted_iota(jnp.int32, (4, 128), 1)
-    lines[9][...] = jnp.sum(jnp.where(diagonal, ratio, 0.0), axis=0, keepdims=True)
-    store(lines[9], rm)
+    for i in range(4):
+        rm[i] = ratio[i, 0]
     for i, dst in enumerate((out, gt, qkv, o, f1, f2)):
         loads[i].wait()
         store(bufs[i], dst)
@@ -730,16 +729,16 @@
     line = sds((width,), F32)
     shapes = (
         sds(out.shape, BF), sds(gt.shape, BF), line, line, sds(qkv.shape, F32), line, line, sds(o.shape, F32), line, line, line,
-        sds(f1.shape, F32), sds((hid,), F32), sds(f2.shape, F32), line, sds((1, 128), F32),
+        sds(f1.shape, F32), sds((hid,), F32), sds(f2.shape, F32), line, sds((4,), F32),
     )
     args = (out, gt, qkv, o, f1, f2, vec, late)
     return pl.pallas_call(
         finish,
         out_shape=shapes,
         in_specs=[any_spec()] * 8,
-        out_specs=(any_spec(),) * 16,
+        out_specs=(any_spec(),) * 15 + (pl.BlockSpec(memory_space=pltpu.SMEM),),
         scratch_shapes=[pltpu.VMEM(v.shape, v.dtype) for v in args] + [pltpu.VMEM((width,), F32)] * 8
-        + [pltpu.VMEM((hid,), F32), pltpu.VMEM((1, 128), F32), pltpu.SemaphoreType.DMA((24,))],
+        + [pltpu.VMEM((hid,), F32), pltpu.SemaphoreType.DMA((24,))],
         name="finish",
     )(*args)
 
@@ -1012,7 +1011,6 @@
     r = list(call_finish(out, gt, qg, og, f1, f2, vec, late, fc1_weight.shape[1]))
     r[0] = r[0][None]
     r[1] = r[1][None]
-    r[15] = r[15][0, :4]
     return tuple(r)
 
 

time: 108 us -> 107 us (level)
  local copies, waits for them, and re-layouts: 1.11 us -> 0 us
    squeeze x1 -> x0, local copies, waits for them, and re-layouts: 1.11 us -> none  [on_device(): r[15] = r[15][0, :4]]
where the time goes in v4:
time: 107 us; the launch traced here: 106 us
  Pallas kernels  105 us (98%)
    pallas_call x1, Pallas kernels, call_everything(): pl.pallas_call(everything, out_shape=(sds((rows, width), BF), sds((rows,...  101 us
    pallas_call x1, Pallas kernels, call_finish(): pl.pallas_call(finish, out_shape=shapes, in_specs=[any_spec()] * 8, out_s...  3.84 us

profile of v4, /device:TPU:0, one launch (start us, length us, event | category | flops | bytes accessed | tf_op | source)
XLA Modules:
  0.0 105.8 jit_solution(12213955604852867424)
XLA Ops:
  0.7 101.2 %everything.1 = (bf16[512,768]{1,0:T(8,128)(2,1)}, bf16[512,768]{1,0:T(8,128)(2,1)}, f32[48,1152]{1,0:T(8,128)}, f32[48,384]{1,0:T(8,128)}, f32[48,1536]{1,0:T(8...) custom-call(bf16[512,768]{1,0:T(8,128)(2,1)} %bitcast.4, s32[1,1024]{1,0:T(1,128)} %seg_hbm.1, ...), custom_call_target="tpu_custom_call" | custom-call | tf_op jit(solution)/shard_map/everything/pallas_call | solution.py:661
  101.8 3.8 %finish.1 = (bf16[512,768]{1,0:T(8,128)(2,1)}, bf16[512,768]{1,0:T(8,128)(2,1)}, f32[768]{0:T(1024)}, f32[768]{0:T(1024)}, f32[48,1152]{1,0:T(8,128)}, /*index=5...) custom-call(bf16[512,768]{1,0:T(8,128)(2,1)} %get-tuple-element.40.r, ...), custom_call_target="tpu_custom_call" | custom-call | tf_op jit(solution)/shard_map/finish/pallas_call | solution.py:735

commit v5 on v4

--- a/solution.py
+++ b/solution.py
@@ -283,7 +283,7 @@
         got_w.append(fetch(w1_hbm.at[:, pl.ds(c * cols, cols)], w1.at[:, pl.ds(c * cols, cols)], 6 + 2 * c))
         got_w.append(fetch(w2_hbm.at[pl.ds(c * cols, cols)], w2.at[pl.ds(c * cols, cols)], 7 + 2 * c))
     project(0, rows, (0, 1, 2))
-    lax.fori_loop(0, heads // 2, attend_far, 0, unroll=3)
+    lax.fori_loop(0, heads // 2, attend_far, 0, unroll=6)
     lax.fori_loop(0, heads // 2, attend_near, 0, unroll=3)
     token_halo.wait()
     normalize(xn, xn, rows, half)
@@ -418,7 +418,7 @@
         add_vec(vec, 6, low.astype(F32))
         return 0
 
-    lax.fori_loop(0, rows // rb, middle, 0)
+    lax.fori_loop(0, rows // rb, middle, 0, unroll=2)
     d_att[own_rows, :] = mm_nt(n2[...], ow[...]).astype(BF)
     mine = jnp.where((lane_at >= head_row) & (lane_at < head_row + HEAD_DIM), 1.0, 0.0).astype(BF)
     prod = d_att[own_rows, :].astype(F32) * att[...].astype(F32)

time: 107 us -> 107 us (level)
  no operation moved by 1% of the time
where the time goes in v5:
time: 107 us; the launch traced here: 106 us
  Pallas kernels  105 us (98%)
    pallas_call x1, Pallas kernels, call_everything(): pl.pallas_call(everything, out_shape=(sds((rows, width), BF), sds((rows,...  102 us
    pallas_call x1, Pallas kernels, call_finish(): pl.pallas_call(finish, out_shape=shapes, in_specs=[any_spec()] * 8, out_s...  3.84 us

profile of v5, /device:TPU:0, one launch (start us, length us, event | category | flops | bytes accessed | tf_op | source)
XLA Modules:
  0.0 106.3 jit_solution(10759276614604053230)
XLA Ops:
  0.7 101.6 %everything.1 = (bf16[512,768]{1,0:T(8,128)(2,1)}, bf16[512,768]{1,0:T(8,128)(2,1)}, f32[48,1152]{1,0:T(8,128)}, f32[48,384]{1,0:T(8,128)}, f32[48,1536]{1,0:T(8...) custom-call(bf16[512,768]{1,0:T(8,128)(2,1)} %bitcast.4, s32[1,1024]{1,0:T(1,128)} %seg_hbm.1, ...), custom_call_target="tpu_custom_call" | custom-call | tf_op jit(solution)/shard_map/everything/pallas_call | solution.py:661
  102.3 3.8 %finish.1 = (bf16[512,768]{1,0:T(8,128)(2,1)}, bf16[512,768]{1,0:T(8,128)(2,1)}, f32[768]{0:T(1024)}, f32[768]{0:T(1024)}, f32[48,1152]{1,0:T(8,128)}, /*index=5...) custom-call(bf16[512,768]{1,0:T(8,128)(2,1)} %get-tuple-element.40.r, ...), custom_call_target="tpu_custom_call" | custom-call | tf_op jit(solution)/shard_map/finish/pallas_call | solution.py:735
